TPU v7x, 32 devices: a whole 2x2x4 slice. The times are simulated.
32 devices in a mesh: stn: 8 (over z, x), grp: 4 (over y, core).
Axes of the slice: x: 2, y: 2, z: 4, core: 2. Of those that a mesh axis runs over, the one named last changes fastest.
Arguments:
- voltages: bfloat16 [2, 16, 2, 180224], P(None, 'stn', None, 'grp'), may hold values from -6 to 6
- corr_taps: float32 [12, 4096], replicated, may hold values from -1.75 to 1.75
- beam_taps: float32 [12, 256], replicated, may hold values from -1.75 to 1.75
- angle_table: float32 [64, 256], replicated, may hold values from -3.140625 to 3.140625
- table_index: int32 [16, 16], replicated, may hold values from 0 to 63
Outputs:
- visibility: float32 [8, 32, 2, 32], P('stn', 'grp')
- beam_power: float32 [256, 16, 704], P('stn', None, 'grp')
All inputs are finite; a program needn't handle non-finite values.
Results may differ from a plain program's by a relative error of at most 0.0046.
Values may be sent and summed in bfloat16 or wider, within the bound.
No kernel may reach another device: no remote copies, remote signals or barrier semaphores. Data moves between devices by JAX's collectives and lax.ppermute only.
A program may use at most 128 MiB of HBM per device.

v0:
```python
import math

import jax
import jax.numpy as jnp
from jax import lax
from jax.sharding import PartitionSpec as P

RADIX = 64


def from_behind(array, axis, by):
    devices = lax.axis_size(axis)
    pairs = [(i, i + by) for i in range(devices) if 0 <= i + by < devices]
    return lax.ppermute(array, axis, pairs)


def dft_tables(length):
    positions = jnp.arange(length, dtype=jnp.int32)
    phases = (positions[:, None] * positions[None, :] % length).astype(jnp.float32) * (
        2.0 * math.pi / length
    )
    factor = 1.0 / math.sqrt(length)
    return (
        (jnp.cos(phases) * factor).astype(jnp.bfloat16),
        (jnp.sin(phases) * factor).astype(jnp.bfloat16),
    )


def twiddles(radix_size):
    positions = jnp.arange(radix_size, dtype=jnp.int32)
    whole = radix_size * radix_size
    phases = (positions[:, None] * positions[None, :] % whole).astype(jnp.float32) * (
        2.0 * math.pi / whole
    )
    return (jnp.cos(phases), jnp.sin(phases))


def polyphase(extended, coefficients, frame_count):
    tap_count, length = coefficients.shape
    shaped = extended.reshape(extended.shape[:-1] + (frame_count + tap_count - 1, length))
    summed = jnp.zeros(shaped.shape[:-2] + (frame_count, length), jnp.float32)
    for tap_index in range(tap_count):
        lead_frame = tap_count - 1 - tap_index
        summed = (
            summed
            + shaped[..., lead_frame : lead_frame + frame_count, :].astype(jnp.float32)
            * coefficients[tap_index]
        )
    return summed.astype(jnp.bfloat16)


def contract(pattern, left_side, right_side):
    return jnp.einsum(pattern, left_side, right_side, preferred_element_type=jnp.float32)


def long_transform(real_part, imag_part):
    cos_table, sin_table = dft_tables(RADIX)
    twist_cos, twist_sin = twiddles(RADIX)
    split_shape = real_part.shape[:-1] + (RADIX, RADIX)
    real_part = real_part.reshape(split_shape)
    imag_part = imag_part.reshape(split_shape)
    first_form = "...ab,ak->...kb"
    middle_real = contract(first_form, real_part, cos_table) + contract(
        first_form, imag_part, sin_table
    )
    middle_imag = contract(first_form, imag_part, cos_table) - contract(
        first_form, real_part, sin_table
    )
    twisted_real = (middle_real * twist_cos + middle_imag * twist_sin).astype(jnp.bfloat16)
    twisted_imag = (middle_imag * twist_cos - middle_real * twist_sin).astype(jnp.bfloat16)
    second_form = "...kb,bm->...mk"
    result_real = contract(second_form, twisted_real, cos_table) + contract(
        second_form, twisted_imag, sin_table
    )
    result_imag = contract(second_form, twisted_imag, cos_table) - contract(
        second_form, twisted_real, sin_table
    )
    flat_shape = split_shape[:-2] + (RADIX * RADIX,)
    return jnp.stack(
        [
            result_real.astype(jnp.bfloat16).reshape(flat_shape),
            result_imag.astype(jnp.bfloat16).reshape(flat_shape),
        ],
        0,
    )


def short_transform(real_part, imag_part):
    cos_table, sin_table = dft_tables(real_part.shape[-1])
    pattern = "...n,nk->...k"
    result_real = contract(pattern, real_part, cos_table) + contract(pattern, imag_part, sin_table)
    result_imag = contract(pattern, imag_part, cos_table) - contract(pattern, real_part, sin_table)
    return jnp.stack([result_real.astype(jnp.bfloat16), result_imag.astype(jnp.bfloat16)], 0)


def station_weights(index_rows, columns, station_total):
    table_rows = jnp.arange(columns.shape[0], dtype=jnp.int32)
    one_hot = (index_rows[..., None] == table_rows).astype(jnp.float32)
    angles = jnp.einsum("bst,tc->bsc", one_hot, columns, precision=lax.Precision.HIGHEST)
    factor = 1.0 / math.sqrt(station_total)
    return (
        (jnp.cos(angles) * factor).astype(jnp.bfloat16),
        (jnp.sin(angles) * factor).astype(jnp.bfloat16),
    )


def beam_terms(weight_real, weight_imag, spec_real, spec_imag):
    pattern = "bsc,sptc->cpbt"
    real_part = contract(pattern, weight_real, spec_real) - contract(
        pattern, weight_imag, spec_imag
    )
    imag_part = contract(pattern, weight_real, spec_imag) + contract(
        pattern, weight_imag, spec_real
    )
    return jnp.stack([real_part, imag_part], 1)


def on_device(voltages, corr_taps, beam_taps, angle_table, table_index):
    tap_count = corr_taps.shape[0]
    length = corr_taps.shape[1]
    short_length = beam_taps.shape[1]
    local_stations = voltages.shape[1]
    samples = voltages.shape[3]
    station_total = local_stations * lax.axis_size("stn")
    history = from_behind(voltages, "grp", 1)
    extended = jnp.concatenate([history, voltages], 3)
    filtered = polyphase(extended, corr_taps, samples // length)
    spectra = long_transform(filtered[0], filtered[1])
    short_input = extended[..., (tap_count - 1) * (length - short_length) :]
    short_filtered = polyphase(short_input, beam_taps, samples // short_length)
    short_spectra = short_transform(short_filtered[0], short_filtered[1])
    owned_channels = short_length // lax.axis_size("stn")
    turned, short_turned = (
        lax.all_to_all(spectra, "stn", split_axis=4, concat_axis=1, tiled=True),
        lax.all_to_all(short_spectra, "stn", split_axis=4, concat_axis=1, tiled=True),
    )
    columns = lax.dynamic_slice_in_dim(
        angle_table, lax.axis_index("stn") * owned_channels, owned_channels, 1
    )
    weight_real, weight_imag = station_weights(table_index, columns, station_total)
    beam_fields = beam_terms(weight_real, weight_imag, short_turned[0], short_turned[1])
    beam_power = jnp.sum(beam_fields[:, 0] ** 2 + beam_fields[:, 1] ** 2, axis=1)
    signals = turned.shape[1] * turned.shape[2]
    inner_depth = turned.shape[3] * turned.shape[4]
    flat_real = turned[0].reshape(signals, inner_depth)
    flat_imag = turned[1].reshape(signals, inner_depth)
    stacked = jnp.concatenate([flat_real, flat_imag], 1)
    rotated = jnp.concatenate([flat_imag, -flat_real], 1)
    real_part = lax.dot_general(
        stacked, stacked, (((1,), (1,)), ((), ())), preferred_element_type=jnp.float32
    )
    imag_part = lax.dot_general(
        rotated, stacked, (((1,), (1,)), ((), ())), preferred_element_type=jnp.float32
    )
    summed = lax.psum_scatter(
        jnp.stack([real_part, imag_part], 1), "grp", scatter_dimension=0, tiled=True
    )
    visibility = (summed * (1.0 / math.sqrt(inner_depth * lax.axis_size("grp"))))[None]
    return (visibility, beam_power)


def solution(mesh):
    in_specs = (P(None, "stn", None, "grp"), P(), P(), P(), P())
    out_specs = (P("stn", "grp", None, None), P("stn", None, "grp"))
    return jax.shard_map(
        on_device, mesh=mesh, in_specs=in_specs, out_specs=out_specs, check_vma=False
    )
```

profile of v0, /device:TPU:0, one launch (start us, length us, event | category | flops | bytes accessed | tf_op | source)
XLA Modules:
  0.0 171.8 jit_solution(5516670431758649028)
XLA Ops:
  7.2 2.6 %collective-permute-start = (bf16[2,2,2,45056]{3,2,1,0:T(2,128)(2,1)}, bf16[2,2,2,45056]{3,2,1,0:T(2,128)(2,1)S(1)}, u32[]{:S(2)}, u32[]{:S(2)}) collective-permute-start(bf16[2,2,2,45056]{3,2,1,0:T(2,128)(2,1)} %param.5), channel_id=1, source_target_pairs={{0,1},{1,2},{2,3},{4,5},{5,6},{6,7},{8,9},{9,10},{10,11},{12,13},{... | collective-permute-start | bytes 2162696 | tf_op jit(solution)/shard_map/ppermute | solution.py:14
  10.1 1.6 fusion.131
  11.8 1.9 %fusion.130 = (f32[1,4096]{1,0:T(1,128)S(1)}, f32[1,4096]{1,0:T(1,128)S(1)}, f32[1,4096]{1,0:T(1,128)S(1)}, f32[1,4096]{1,0:T(1,128)S(1)}, f32[1,4096]{1,0:T(1,1...) fusion(f32[12,4096]{1,0:T(8,128)} %param.6), kind=kLoop, calls=%fused_computation.158 | loop fusion | bytes 393216 | tf_op jit(solution)/shard_map/slice | solution.py:47
  14.8 1.4 slice.248
  17.3 1.5 reshape.80
  18.9 2.3 %add_convert_fusion.1 = bf16[2,2,2,176,256]{4,3,2,1,0:T(8,128)(2,1)S(1)} fusion(bf16[2,2,2,187,256]{4,3,2,1,0:T(8,128)(2,1)S(1)} %reshape.80, f32[256]{0:T(256)S(1)} %bitcast.165, f32[256]{0:T(256)S(1)} %bitcast.166, f32[256]{0:T(256)S(1)} %bitcast.156, f32[256]{0:T(256)S(1)} %bitcast.157, f32[256]{0:T(256)S(1)} %bitcast.158, f32[256]{0:T(256)S(1)} %bitcast.159, ...), kind=kLoop, calls=%fused_computation.5 | loop fusion | flops 12976128 | bytes 9383936 | tf_op jit(solution)/shard_map/convert_element_type | solution.py:49
  21.2 2.1 %fusion.18 = f32[2,2,176,256]{3,2,1,0:T(8,128)} fusion(bf16[2,2,2,176,256]{4,3,2,1,0:T(8,128)(2,1)S(1)} %add_convert_fusion.1), kind=kOutput, calls=%fused_computation.39 | convolution fusion | flops 93323264 | bytes 1081344 | tf_op jit(solution)/shard_map/...n,nk->...k/dot_general | solution.py:53
  23.2 2.1 %fusion.17 = f32[2,2,176,256]{3,2,1,0:T(8,128)} fusion(bf16[2,2,2,176,256]{4,3,2,1,0:T(8,128)(2,1)S(1)} %add_convert_fusion.1), kind=kOutput, calls=%fused_computation.38 | convolution fusion | flops 93323264 | bytes 1081344 | tf_op jit(solution)/shard_map/...n,nk->...k/dot_general | solution.py:53
  25.3 3.2 %add_convert_fusion = bf16[2,2,2,11,4096]{4,3,2,1,0:T(8,128)(2,1)S(1)} fusion(bf16[2,2,2,22,4096]{4,3,2,1,0:T(8,128)(2,1)S(1)} %reshape.79, f32[4096]{0:T(1024)S(1)} %bitcast.153, f32[4096]{0:T(1024)S(1)} %bitcast.154, f32[4096]{0:T(1024)S(1)} %bitcast.144, f32[4096]{0:T(1024)S(1)} %bitcast.145, f32[4096]{0:T(1024)S(1)} %bitcast.146, f32[4096]{0:T(1024)S(1)} %bitcast.147, ...), kind=kLoop, calls=%fused_computation | loop fusion | flops 12976128 | bytes 9568256 | tf_op jit(solution)/shard_map/convert_element_type | solution.py:49
  30.2 2.4 %fusion.10 = bf16[1,2,2,176,256]{4,3,2,1,0:T(8,128)(2,1)S(1)} fusion(f32[2,2,176,256]{3,2,1,0:T(8,128)} %fusion.18, bf16[2,2,2,176,256]{4,3,2,1,0:T(8,128)(2,1)S(1)} %add_convert_fusion.1), kind=kOutput, calls=%fused_computation.22 | convolution fusion | flops 93683712 | bytes 1441792 | tf_op jit(solution)/shard_map/...n,nk->...k/dot_general | solution.py:53
  32.6 1.2 fusion.11
  33.9 2.1 %copy.76 = bf16[2,2,2,176,256]{3,2,1,0,4:T(2,128)(2,1)} copy(bf16[2,2,2,176,256]{4,3,2,1,0:T(8,128)(2,1)S(1)} %pad_maximum_fusion.1) | data formatting | bytes 1441792 | tf_op jit(solution)/shard_map/stack | solution.py:93
  36.0 6.6 %all-to-all-start.1 = ((bf16[2,2,2,176,256]{3,2,1,0,4:T(2,128)(2,1)}), bf16[2,2,2,176,256]{3,2,1,0,4:T(2,128)(2,1)S(1)}, u32[]{:S(2)}, u32[]{:S(2)}) async-start(bf16[2,2,2,176,256]{3,2,1,0,4:T(2,128)(2,1)} %copy.76), calls=%async_computation.2 | async-start | bytes 2097152 | tf_op jit(solution)/shard_map/all_to_all | solution.py:135
  46.4 1.5 reshape.90
  47.9 2.2 %copy.94 = bf16[1,2,2,11,4096]{4,2,3,1,0:T(2,128)(2,1)} copy(bf16[1,2,2,11,4096]{4,3,2,1,0:T(8,128)(2,1)} %reshape.90) | data formatting | bytes 720896 | tf_op jit(solution)/shard_map/stack;reshape | solution.py:79
  53.9 14.5 %copy.72 = bf16[2,2,2,11,4096]{3,2,1,0,4:T(2,128)(2,1)} copy(bf16[2,2,2,11,4096]{4,2,3,1,0:T(2,128)(2,1)S(1)} %pad_maximum_fusion) | data formatting | bytes 1441792 | tf_op jit(solution)/shard_map/stack | solution.py:79
  68.4 13.9 %reshape.94 = bf16[8,2,22528]{2,1,0:T(2,128)(2,1)} reshape(bf16[4096,2,2,2,11]{4,3,2,1,0:T(2,128)(2,1)} %bitcast.133) | data formatting | bytes 1441792
  82.3 6.1 %all-to-all-start = ((bf16[8,2,22528]{2,1,0:T(2,128)(2,1)}), bf16[8,2,22528]{2,1,0:T(2,128)(2,1)}, u32[]{:S(2)}, u32[]{:S(2)}) async-start(bf16[8,2,22528]{2,1,0:T(2,128)(2,1)} %reshape.94), calls=%async_computation | async-start | bytes 1441792 | tf_op jit(solution)/shard_map/all_to_all | solution.py:134
  92.7 10.1 %all-to-all-done = bf16[8,2,22528]{2,1,0:T(2,128)(2,1)} async-done(((bf16[8,2,22528]{2,1,0:T(2,128)(2,1)}), bf16[8,2,22528]{2,1,0:T(2,128)(2,1)}, u32[]{:S(2)}, u32[]{:S(2)}) %all-to-all-start) | async-done | bytes 720928 | tf_op jit(solution)/shard_map/all_to_all | solution.py:134
  102.9 20.6 %reshape.95 = bf16[4096,2,2,2,11]{4,3,2,1,0:T(2,128)(2,1)} reshape(bf16[8,2,22528]{2,1,0:T(2,128)(2,1)} %all-to-all-done) | data formatting | bytes 1441792
  123.5 12.9 %copy.96 = bf16[2,2,2,11,8,512]{5,4,2,3,1,0:T(8,128)(2,1)} copy(bf16[2,2,2,11,8,512]{3,2,1,0,5,4:T(2,128)(2,1)} %bitcast.134) | data formatting | bytes 1441792 | tf_op jit(solution)/shard_map/all_to_all | solution.py:134
  136.4 1.1 fusion.128
  140.1 1.1 fusion.5
  141.2 22.5 %reduce-scatter.2.cloned.1.call-done = f32[8,2,32]{2,0,1:T(8,128)} async-done(((f32[32,2,32]{2,0,1:T(8,128)}), f32[8,2,32]{2,0,1:T(8,128)}) %reduce-scatter.2.cloned.1.call-update) | async-done | bytes 2064 | tf_op jit(solution)/shard_map/reduce_scatter | solution.py:155
  (75 shorter events, 19.7 us)
Async XLA Ops:
  7.2 81.6 %copy-start = (f32[64,256]{1,0:T(8,128)S(1)}, f32[64,256]{1,0:T(8,128)}, u32[]{:S(2)}) copy-start(f32[64,256]{1,0:T(8,128)} %param.8) | copy-start | bytes 196612
  7.2 7.1 %copy-start.2 = (bf16[2,2,2,45056]{3,2,1,0:T(2,128)(2,1)S(1)}, bf16[2,2,2,45056]{3,2,1,0:T(2,128)(2,1)}, u32[]{:S(2)}) copy-start(bf16[2,2,2,45056]{3,2,1,0:T(2,128)(2,1)} %param.5) | copy-start | bytes 2162692
  7.2 6.6 %collective-permute-start = (bf16[2,2,2,45056]{3,2,1,0:T(2,128)(2,1)}, bf16[2,2,2,45056]{3,2,1,0:T(2,128)(2,1)S(1)}, u32[]{:S(2)}, u32[]{:S(2)}) collective-permute-start(bf16[2,2,2,45056]{3,2,1,0:T(2,128)(2,1)} %param.5), channel_id=1, source_target_pairs={{0,1},{1,2},{2,3},{4,5},{5,6},{6,7},{8,9},{9,10},{10,11},{12,13},{... | collective-permute-start | bytes 2162696 | tf_op jit(solution)/shard_map/ppermute | solution.py:14
  17.2 1.6 copy-start.3
  17.2 1.6 copy-start.4
  17.2 1.6 copy-start.5
  17.2 1.6 copy-start.6
  17.2 1.6 copy-start.7
  17.2 1.6 copy-start.8
  17.2 1.6 copy-start.9
  17.2 1.6 copy-start.10
  30.2 2.4 %copy-start.12 = (f32[2,2,176,256]{3,2,1,0:T(8,128)S(1)}, f32[2,2,176,256]{3,2,1,0:T(8,128)}, u32[]{:S(2)}) copy-start(f32[2,2,176,256]{3,2,1,0:T(8,128)} %fusion.17) | copy-start | bytes 2162692
  36.0 46.3 %all-to-all-start.1 = ((bf16[2,2,2,176,256]{3,2,1,0,4:T(2,128)(2,1)}), bf16[2,2,2,176,256]{3,2,1,0,4:T(2,128)(2,1)S(1)}, u32[]{:S(2)}, u32[]{:S(2)}) async-start(bf16[2,2,2,176,256]{3,2,1,0,4:T(2,128)(2,1)} %copy.76), calls=%async_computation.2 | async-start | bytes 2097152 | tf_op jit(solution)/shard_map/all_to_all | solution.py:135
  51.7 1.1 copy-start.1
  82.3 6.4 %copy-start.11 = (s32[16,16]{1,0:T(8,128)S(1)}, s32[16,16]{1,0:T(8,128)}, u32[]{:S(2)}) copy-start(s32[16,16]{1,0:T(8,128)} %param.9) | copy-start | bytes 3076
  82.3 20.6 %all-to-all-start = ((bf16[8,2,22528]{2,1,0:T(2,128)(2,1)}), bf16[8,2,22528]{2,1,0:T(2,128)(2,1)}, u32[]{:S(2)}, u32[]{:S(2)}) async-start(bf16[8,2,22528]{2,1,0:T(2,128)(2,1)} %reshape.94), calls=%async_computation | async-start | bytes 1441792 | tf_op jit(solution)/shard_map/all_to_all | solution.py:134
  88.4 75.2 %reduce-scatter.2.cloned.1.call-start = ((), (), s32[]{:S(2)}) async-start(), calls=%async_computation.3 | async-start | bytes 40960 | tf_op jit(solution)/shard_map/reduce_scatter | solution.py:155
Sparse Core Ops, SparseCore 0:
  139.9 23.7 reduce-scatter.1
where the time goes:
time: 173 us; the launch traced here: 172 us
  local copies, waits for them, and re-layouts  84.3 us (49%)
  waiting for transfers between devices  32.7 us (19%)
  matrix products  16.5 us (10%)
  starting transfers between devices  15.6 us (9%)
  between operations  14.5 us (8%)
  other arithmetic  8.26 us (5%)
    unnamed x32, local copies, waits for them, and re-layouts  36.2 us
    reduce_scatter x1, waiting for transfers between devices, on_device(): lax.psum_scatter(jnp.stack([real_part, imag_part], 1), 'grp', scatter_dim...  22.5 us
    another operation x5, local copies, waits for them, and re-layouts, long_transform(): jnp.stack([result_real.astype(jnp.bfloat16).reshape(flat_shape), result_i...  19.2 us
    dot_general x16, matrix products, contract(): jnp.einsum(pattern, left_side, right_side, preferred_element_type=jnp.flo...  15.1 us
    all_to_all x1, local copies, waits for them, and re-layouts, on_device(): lax.all_to_all(spectra, 'stn', split_axis=4, concat_axis=1, tiled=True)  12.9 us
    all_to_all x1, waiting for transfers between devices, on_device(): lax.all_to_all(spectra, 'stn', split_axis=4, concat_axis=1, tiled=True)  10.1 us
    all_to_all x1, starting transfers between devices, on_device(): lax.all_to_all(short_spectra, 'stn', split_axis=4, concat_axis=1, tiled=T...  6.62 us
    all_to_all x1, starting transfers between devices, on_device(): lax.all_to_all(spectra, 'stn', split_axis=4, concat_axis=1, tiled=True)  6.14 us
  transfers between devices with their start and end apart: 4, of which 2 were waited for; matrix products, arithmetic and copies ran while one was open for 28% of the time, Pallas kernels for 0%

commit v1 on v0

v1 whole, which is shorter than its diff:
```python
import functools
import math

import jax
import jax.numpy as jnp
import numpy as np
from jax import lax
from jax.experimental import pallas as pl
from jax.experimental.pallas import tpu as pltpu
from jax.sharding import PartitionSpec as P

LANES = 128
GROUPS = 8


def from_behind(array, axis, by):
    devices = lax.axis_size(axis)
    pairs = [(i, i + by) for i in range(devices) if 0 <= i + by < devices]
    return lax.ppermute(array, axis, pairs)


def dft_tables(rows, columns):
    length = max(rows, columns)
    phases = (np.arange(rows)[:, None] * np.arange(columns)[None, :] % length) * (2.0 * np.pi / length)
    return np.cos(phases) / math.sqrt(length), np.sin(phases) / math.sqrt(length)


def pulsar_table(length):
    cos_table, sin_table = dft_tables(length, length)
    return np.concatenate([cos_table, sin_table], 1)


def block_stage_table(blocks, pairs):
    cos_table, sin_table = dft_tables(blocks, blocks)
    real_row = np.stack([cos_table, sin_table], 0)
    imag_row = np.stack([-sin_table, cos_table], 0)
    parts = np.stack([np.stack([real_row, imag_row], 0), np.stack([imag_row, -real_row], 0)], 0)
    parts = parts.reshape(2, 2, 2, blocks, blocks // GROUPS, GROUPS)
    full = np.einsum("aorbqi,sp->aiqosrpb", parts, np.eye(pairs))
    return full.reshape(2 * blocks * 2 * pairs, 2 * pairs * blocks)


def lane_stage_table():
    cos_table, sin_table = dft_tables(LANES, LANES)
    table = np.concatenate([cos_table, sin_table], 0)
    width = LANES // GROUPS
    return np.concatenate([np.roll(table, i * width, 1) for i in range(GROUPS)], 1)


def twiddle_tables(blocks, repeats):
    order = np.arange(blocks).reshape(blocks // GROUPS, GROUPS).T.reshape(-1)
    phases = (order[:, None] * np.arange(LANES)[None, :]) * (2.0 * np.pi / (blocks * LANES))
    phases = np.repeat(phases, repeats, 0)
    return np.cos(phases).astype(np.float32), np.sin(phases).astype(np.float32)


def dot(left_side, right_side):
    return jnp.dot(left_side, right_side, preferred_element_type=jnp.float32)


def dot_rows(left_side, right_side):
    return lax.dot_general(
        left_side, right_side, (((1,), (1,)), ((), ())), preferred_element_type=jnp.float32
    )


def pulsar_kernel(history_ref, own_ref, taps_ref, table_ref, out_ref, wide, summed, stacked):
    rows = own_ref.shape[0]
    taps, length = taps_ref.shape
    parts = length // LANES
    frames = own_ref.shape[1] // length
    past = history_ref.shape[1] // LANES
    for block in range(past):
        wide[block] = history_ref[:, block * LANES : (block + 1) * LANES].astype(jnp.float32)

    def widen(step, carry):
        at = pl.multiple_of(step * (16 * LANES), 16 * LANES)
        piece = own_ref[:, pl.ds(at, 16 * LANES)]
        for j in range(16):
            wide[past + step * 16 + j] = piece[:, j * LANES : (j + 1) * LANES].astype(jnp.float32)
        return carry

    lax.fori_loop(0, own_ref.shape[1] // LANES // 16, widen, 0)
    chunk = 16
    for part in range(parts):
        weights = [
            jnp.broadcast_to(taps_ref[k : k + 1, part * LANES : (part + 1) * LANES], (rows, LANES))
            for k in range(taps)
        ]

        def filter_frames(step, carry):
            first = step * chunk
            values = [wide[(first + j) * parts + part] for j in range(chunk + taps - 1)]
            for j in range(chunk):
                total = values[j + taps - 1] * weights[0]
                for k in range(1, taps):
                    total = total + values[j + taps - 1 - k] * weights[k]
                summed[part, pl.ds(first + j, rows, stride=frames), :] = total
            return carry

        lax.fori_loop(0, frames // chunk, filter_frames, 0)
    half = rows * frames // 2

    def stack(step, carry):
        at = pl.multiple_of(step * 64, 64)
        for part in range(parts):
            real_part = summed[part, pl.ds(at, 64), :].astype(jnp.bfloat16)
            imag_part = summed[part, pl.ds(at + half, 64), :].astype(jnp.bfloat16)
            low = slice(part * LANES, (part + 1) * LANES)
            high = slice(length + part * LANES, length + (part + 1) * LANES)
            stacked[pl.ds(at, 64), low] = real_part
            stacked[pl.ds(at, 64), high] = imag_part
            stacked[pl.ds(at + half, 64), low] = imag_part
            stacked[pl.ds(at + half, 64), high] = -real_part
        return carry

    lax.fori_loop(0, half // 64, stack, 0)
    out_ref[...] = dot_rows(table_ref[...], stacked[...]).astype(jnp.bfloat16)


def pulsar_spectra(history, own, taps):
    rows, samples = own.shape
    length = taps.shape[1]
    frames = samples // length
    table = jnp.asarray(pulsar_table(length), jnp.bfloat16)
    blocks = (history.shape[1] + samples) // LANES
    return pl.pallas_call(
        pulsar_kernel,
        out_shape=jax.ShapeDtypeStruct((length, rows * frames), jnp.bfloat16),
        scratch_shapes=[
            pltpu.VMEM((blocks, rows, LANES), jnp.float32),
            pltpu.VMEM((length // LANES, rows * frames, LANES), jnp.float32),
            pltpu.VMEM((rows * frames, 2 * length), jnp.bfloat16),
        ],
        cost_estimate=pl.CostEstimate(flops=600000000, bytes_accessed=2000000, transcendentals=0),
        name="pulsar_spectra",
    )(history, own, taps, table)


def correlator_kernel(history_ref, own_ref, taps_ref, first_ref, second_ref, cos_ref, sin_ref, out_ref, wide, summed, twisted, mixed):
    rows = own_ref.shape[0]
    taps, length = taps_ref.shape
    blocks = length // LANES
    frames = own_ref.shape[1] // length
    past = taps - 1
    for ref, start in ((history_ref, 0), (own_ref, past * blocks)):

        def widen(step, carry, ref=ref, start=start):
            at = pl.multiple_of(step * (16 * LANES), 16 * LANES)
            piece = ref[:, pl.ds(at, 16 * LANES)]
            for j in range(16):
                wide[start + step * 16 + j] = piece[:, j * LANES : (j + 1) * LANES].astype(jnp.float32)
            return carry

        lax.fori_loop(0, ref.shape[1] // LANES // 16, widen, 0)

    def filter_block(block, carry):
        at = pl.multiple_of(block * LANES, LANES)
        weights = [
            jnp.broadcast_to(taps_ref[k : k + 1, pl.ds(at, LANES)], (rows, LANES)) for k in range(taps)
        ]
        values = [wide[frame * blocks + block] for frame in range(frames + past)]
        for frame in range(frames):
            total = values[frame + past] * weights[0]
            for k in range(1, taps):
                total = total + values[frame + past - k] * weights[k]
            summed[frame, pl.ds(block, rows, stride=blocks), :] = total
        return carry

    lax.fori_loop(0, blocks, filter_block, 0)
    height = rows * blocks
    per_group = height // GROUPS

    def transform(frame, carry):
        middle = dot(first_ref[...], summed[frame].astype(jnp.bfloat16))
        left_part, right_part = middle[:height], middle[height:]
        twist_cos, twist_sin = cos_ref[...], sin_ref[...]
        low = (left_part * twist_cos + right_part * twist_sin).astype(jnp.bfloat16)
        high = (right_part * twist_cos - left_part * twist_sin).astype(jnp.bfloat16)
        at = pl.multiple_of(frame * per_group, per_group)
        for i in range(GROUPS):
            here = slice(i * per_group, (i + 1) * per_group)
            twisted[i, pl.ds(at, per_group), :LANES] = low[here]
            twisted[i, pl.ds(at, per_group), LANES:] = high[here]
        return carry

    lax.fori_loop(0, frames, transform, 0)
    for i in range(GROUPS):
        mixed[i] = dot(twisted[i], second_ref[:, i * LANES : (i + 1) * LANES])
    group = lax.broadcasted_iota(jnp.int32, (rows, LANES), 1) // (LANES // GROUPS)

    def gather(step, carry):
        at = pl.multiple_of(step * rows, rows)
        tiles = [mixed[i, pl.ds(at, rows), :] for i in range(GROUPS)]
        for bit in (1, 2, 4):
            pick = (group & bit) != 0
            tiles = [jnp.where(pick, tiles[(i + bit) % GROUPS], tiles[i]) for i in range(GROUPS)]
        lane = pl.multiple_of(step * LANES, LANES)
        for d in range(GROUPS):
            out_ref[d * rows : (d + 1) * rows, pl.ds(lane, LANES)] = tiles[-d % GROUPS].astype(jnp.bfloat16)
        return carry

    lax.fori_loop(0, frames * blocks // GROUPS, gather, 0)


def correlator_spectra(history, own, taps):
    rows, samples = own.shape
    length = taps.shape[1]
    frames = samples // length
    blocks = length // LANES
    first = jnp.asarray(block_stage_table(blocks, rows // 2), jnp.bfloat16)
    second = jnp.asarray(lane_stage_table(), jnp.bfloat16)
    twist_cos, twist_sin = twiddle_tables(blocks, rows)
    height = rows * blocks
    tiles = frames * blocks // GROUPS
    return pl.pallas_call(
        correlator_kernel,
        out_shape=jax.ShapeDtypeStruct((GROUPS * rows, tiles * LANES), jnp.bfloat16),
        scratch_shapes=[
            pltpu.VMEM(((frames + taps.shape[0] - 1) * blocks, rows, LANES), jnp.float32),
            pltpu.VMEM((frames, height, LANES), jnp.float32),
            pltpu.VMEM((GROUPS, frames * height // GROUPS, 2 * LANES), jnp.bfloat16),
            pltpu.VMEM((GROUPS, frames * height // GROUPS, LANES), jnp.float32),
        ],
        cost_estimate=pl.CostEstimate(flops=1000000000, bytes_accessed=4000000, transcendentals=0),
        name="correlator_spectra",
    )(history, own, taps, first, second, jnp.asarray(twist_cos), jnp.asarray(twist_sin))


def beam_kernel(weight_ref, spec_ref, out_ref, stacked):
    sources = spec_ref.shape[0]
    depth = weight_ref.shape[1]
    terms = depth // sources
    width = spec_ref.shape[1] // terms
    for i in range(terms):
        stacked[i * sources : (i + 1) * sources, :] = spec_ref[:, i * width : (i + 1) * width]
    height = weight_ref.shape[0] // 2
    chunk = min(height, 128)
    frames = width // 2

    def form(step, carry):
        at = pl.multiple_of(step * chunk, chunk)
        real_part = dot(weight_ref[pl.ds(at, chunk), :], stacked[...])
        imag_part = dot(weight_ref[pl.ds(height + at, chunk), :], stacked[...])
        power = real_part * real_part + imag_part * imag_part
        out_ref[pl.ds(at, chunk), :] = power[:, :frames] + power[:, frames:]
        return carry

    lax.fori_loop(0, height // chunk, form, 0)


def beam_former(weights, spectra):
    terms = weights.shape[1] // spectra.shape[0]
    width = spectra.shape[1] // terms
    return pl.pallas_call(
        beam_kernel,
        out_shape=jax.ShapeDtypeStruct((weights.shape[0] // 2, width // 2), jnp.float32),
        scratch_shapes=[pltpu.VMEM((weights.shape[1], width), jnp.bfloat16)],
        cost_estimate=pl.CostEstimate(flops=700000000, bytes_accessed=4000000, transcendentals=0),
        name="beam_former",
    )(weights, spectra)


def gram_kernel(spec_ref, out_ref):
    out_ref[...] = dot_rows(spec_ref[...], spec_ref[...])


def gram(spectra):
    rows = spectra.shape[0]
    return pl.pallas_call(
        gram_kernel,
        out_shape=jax.ShapeDtypeStruct((rows, rows), jnp.float32),
        cost_estimate=pl.CostEstimate(flops=50000000, bytes_accessed=1000000, transcendentals=0),
        name="gram",
    )(spectra)


def station_weights(index_rows, columns, station_total):
    table_rows = jnp.arange(columns.shape[0], dtype=jnp.int32)
    one_hot = (index_rows[..., None] == table_rows).astype(jnp.float32)
    angles = jnp.einsum("bst,tc->bsc", one_hot, columns, precision=lax.Precision.HIGHEST)
    factor = 1.0 / math.sqrt(station_total)
    return (
        (jnp.cos(angles) * factor).astype(jnp.bfloat16),
        (jnp.sin(angles) * factor).astype(jnp.bfloat16),
    )


def beam_matrix(weight_real, weight_imag, local_stations):
    beams, stations, channels = weight_real.shape
    parts = jnp.stack(
        [jnp.stack([weight_real, -weight_imag], 0), jnp.stack([weight_imag, weight_real], 0)], 0
    )
    parts = parts.reshape(2, 2, beams, stations // local_stations, local_stations, channels)
    parts = parts.transpose(0, 5, 2, 1, 4, 3)[..., None]
    same = jnp.eye(channels, dtype=jnp.bfloat16).reshape(1, channels, 1, 1, 1, 1, channels)
    return (parts * same).reshape(2 * channels * beams, 2 * stations * channels)


def sum_over_grp(matrix):
    members = lax.axis_size("grp")
    me = lax.axis_index("grp")
    blocks = matrix.reshape(members, matrix.shape[0] // members, matrix.shape[1])
    total = lax.dynamic_index_in_dim(blocks, me, 0, keepdims=False)
    for by in range(1, members):
        away = lax.dynamic_index_in_dim(blocks, (me + by) % members, 0, keepdims=False)
        total = total + lax.ppermute(away, "grp", [(i, (i + by) % members) for i in range(members)])
    return total


def on_device(voltages, corr_taps, beam_taps, angle_table, table_index):
    tap_count = corr_taps.shape[0]
    length = corr_taps.shape[1]
    short_length = beam_taps.shape[1]
    local_stations, polarizations, samples = voltages.shape[1:]
    owners = lax.axis_size("stn")
    station_total = local_stations * owners
    pairs = local_stations * polarizations
    rows = 2 * pairs
    own = voltages.reshape(rows, samples)
    short_past = (tap_count - 1) * short_length
    near = from_behind(own[:, samples - short_past :], "grp", 1)
    past = from_behind(own[:, samples - (tap_count - 1) * length :], "grp", 1)
    short = pulsar_spectra(near, own, beam_taps)
    owned_channels = short_length // owners
    short = short.reshape(owners, owned_channels, short.shape[1])
    short_turned = lax.all_to_all(short, "stn", split_axis=0, concat_axis=0, tiled=True)
    spectra = correlator_spectra(past, own, corr_taps)
    subs = owners // GROUPS
    spectra = spectra.reshape(GROUPS, rows, -1, subs, LANES // GROUPS // subs)
    spectra = spectra.transpose(0, 3, 1, 2, 4).reshape(owners, rows, -1)
    turned = lax.all_to_all(spectra, "stn", split_axis=0, concat_axis=0, tiled=True)
    columns = lax.dynamic_slice_in_dim(
        angle_table, lax.axis_index("stn") * owned_channels, owned_channels, 1
    )
    weight_real, weight_imag = station_weights(table_index, columns, station_total)
    matrix = beam_matrix(weight_real, weight_imag, local_stations)
    beam_power = beam_former(matrix, short_turned.reshape(owners * owned_channels, -1))
    beam_power = beam_power.reshape(owned_channels, table_index.shape[0], -1)
    inner_depth = turned.shape[2]
    products = gram(turned.reshape(owners * rows, inner_depth))
    summed = sum_over_grp(products)
    held = owners // lax.axis_size("grp")
    summed = summed.reshape(held, 2, pairs, owners, 2, pairs)
    real_part = summed[:, 0, :, :, 0] + summed[:, 1, :, :, 1]
    imag_part = summed[:, 1, :, :, 0] - summed[:, 0, :, :, 1]
    signals = owners * pairs
    visibility = jnp.stack(
        [real_part.reshape(held * pairs, signals), imag_part.reshape(held * pairs, signals)], 1
    )
    visibility = (visibility * (1.0 / math.sqrt(inner_depth * lax.axis_size("grp"))))[None]
    return (visibility, beam_power)


def solution(mesh):
    in_specs = (P(None, "stn", None, "grp"), P(), P(), P(), P())
    out_specs = (P("stn", "grp", None, None), P("stn", None, "grp"))
    return jax.shard_map(
        on_device, mesh=mesh, in_specs=in_specs, out_specs=out_specs, check_vma=False
    )
```

time: 173 us -> 83.5 us (0.48)
  local copies, waits for them, and re-layouts: 84.3 us -> 20.4 us
  waiting for transfers between devices: 32.7 us -> 1.77 us
  Pallas kernels: 0 us -> 20.1 us
  matrix products: 16.5 us -> 1.38 us
  between operations: 14.5 us -> 0.77 us
  starting transfers between devices: 15.6 us -> 29.3 us
    unnamed x32 -> x13, local copies, waits for them, and re-layouts: 36.2 us -> 2.98 us
    another operation x8 -> x2, local copies, waits for them, and re-layouts: 22.8 us -> 0.15 us  [on_device(): jnp.stack([real_part.reshape(held * pairs, signals), imag_part.reshape(he...]
    reduce_scatter x1 -> x0, waiting for transfers between devices: 22.5 us -> none  [on_device(): lax.psum_scatter(jnp.stack([real_part, imag_part], 1), 'grp', scatter_dim...]
    pallas_call x0 -> x4, Pallas kernels: none -> 20.1 us  [the longest x1 8.75 us: correlator_spectra(): pl.pallas_call(correlator_kernel, out_shape=jax.ShapeDtypeStruct((GROUPS...]
    dot_general x18 -> x0, matrix products: 15.7 us -> none  [the longest x16 15.1 us: contract(): jnp.einsum(pattern, left_side, right_side, preferred_element_type=jnp.flo...]
    all_to_all x2 -> x0, local copies, waits for them, and re-layouts: 13.1 us -> none  [the longest x1 12.9 us: on_device(): lax.all_to_all(spectra, 'stn', split_axis=4, concat_axis=1, tiled=True)]
    mul x0 -> x1, local copies, waits for them, and re-layouts: none -> 12.4 us  [beam_matrix(): return (parts * same).reshape(2 * channels * beams, 2 * stations * channels)]
    all_to_all x2, waiting for transfers between devices: 10.1 us -> 0.01 us  [the longest x1 0.01 us: on_device(): lax.all_to_all(spectra, 'stn', split_axis=0, concat_axis=0, tiled=True)]
  transfers between devices with their start and end apart: 4 -> 7, of which waited for: 2 -> 1; matrix products, arithmetic and copies ran while one was open for 28% -> 30% of each run, Pallas kernels for 0% -> 14%
where the time goes in v1:
time: 83.5 us; the launch traced here: 82.6 us
  starting transfers between devices  29.3 us (35%)
  local copies, waits for them, and re-layouts  20.4 us (24%)
  Pallas kernels  20.1 us (24%)
  other arithmetic  8.79 us (11%)
  waiting for transfers between devices  1.77 us (2%)
  matrix products  1.38 us (2%)
    mul x1, local copies, waits for them, and re-layouts, beam_matrix(): return (parts * same).reshape(2 * channels * beams, 2 * stations * channels)  12.4 us
    ppermute x2, starting transfers between devices, from_behind(): return lax.ppermute(array, axis, pairs)  12.3 us
    pallas_call x1, Pallas kernels, correlator_spectra(): pl.pallas_call(correlator_kernel, out_shape=jax.ShapeDtypeStruct((GROUPS...  8.75 us
    mul x1, other arithmetic, beam_matrix(): return (parts * same).reshape(2 * channels * beams, 2 * stations * channels)  7 us
    all_to_all x1, starting transfers between devices, on_device(): lax.all_to_all(spectra, 'stn', split_axis=0, concat_axis=0, tiled=True)  6.62 us
    all_to_all x1, starting transfers between devices, on_device(): lax.all_to_all(short, 'stn', split_axis=0, concat_axis=0, tiled=True)  5.72 us
    pallas_call x1, Pallas kernels, beam_former(): pl.pallas_call(beam_kernel, out_shape=jax.ShapeDtypeStruct((weights.shape...  4.84 us
    ppermute x3, starting transfers between devices, sum_over_grp(): lax.ppermute(away, 'grp', [(i, (i + by) % members) for i in range(members)])  4.69 us
  transfers between devices with their start and end apart: 7, of which 1 were waited for; matrix products, arithmetic and copies ran while one was open for 30% of the time, Pallas kernels for 14%

profile of v1, /device:TPU:0, one launch (start us, length us, event | category | flops | bytes accessed | tf_op | source)
XLA Modules:
  0.0 82.6 jit_solution(4178286203668747784)
XLA Ops:
  0.6 1.4 %reshape.132.own_ref = bf16[8,45056]{1,0:T(8,128)(2,1)S(1)} reshape(bf16[2,2,2,45056]{3,2,1,0:T(2,128)(2,1)} %param.10) | data formatting | bytes 1441792 | tf_op jit(solution)/shard_map/reshape | solution.py:320
  2.1 2.4 %collective-permute-start = (bf16[8,45056]{1,0:T(8,128)(2,1)S(1)}, bf16[8,45056]{1,0:T(8,128)(2,1)S(1)}, u32[]{:S(2)}, u32[]{:S(2)}) collective-permute-start(bf16[8,45056]{1,0:T(8,128)(2,1)S(1)} %reshape.132.own_ref), channel_id=1, source_target_pairs={{0,1},{1,2},{2,3},{4,5},{5,6},{6,7},{8,9},{9,10},{10,11},{12,13},{... | collective-permute-start | bytes 2162696 | tf_op jit(solution)/shard_map/ppermute | solution.py:19
  4.5 1.8 %collective-permute-done.history_ref = bf16[8,45056]{1,0:T(8,128)(2,1)S(1)} collective-permute-done((bf16[8,45056]{1,0:T(8,128)(2,1)S(1)}, bf16[8,45056]{1,0:T(8,128)(2,1)S(1)}, u32[]{:S(2)}, u32[]{:S(2)}) %collective-permute-start) | collective-permute-done | bytes 720928 | tf_op jit(solution)/shard_map/ppermute | solution.py:19
  6.3 0.9 %copy-done.4 = bf16[8,45056]{1,0:T(8,128)(2,1)} copy-done((bf16[8,45056]{1,0:T(8,128)(2,1)}, bf16[8,45056]{1,0:T(8,128)(2,1)S(1)}, u32[]{:S(2)}) %copy-start.4) | copy-done | bytes 720920
  7.2 8.8 %correlator_spectra.1 = bf16[64,5632]{1,0:T(8,128)(2,1)} custom-call(bf16[8,45056]{1,0:T(8,128)(2,1)} %copy-done.4, bf16[8,45056]{1,0:T(8,128)(2,1)} %copy-done.3, f32[12,4096]{1,0:T(8,128)} %taps_ref.2, bf16[512,256]{1,0:T(8,128)(2,1)} %constant.65.clone.first_ref, bf16[256,1024]{1,0:T(8,128)(2,1)} %constant.66.clone.second_ref, ...), custom_call_target="tpu_custom_call" | custom-call | flops 1000000000 | bytes 4000000 | tf_op jit(solution)/shard_map/correlator_spectra/pallas_call | solution.py:216
  15.9 6.6 %all-to-all-start = ((bf16[8,8,5632]{2,1,0:T(8,128)(2,1)}), bf16[8,8,5632]{2,1,0:T(8,128)(2,1)S(1)}, u32[]{:S(2)}, u32[]{:S(2)}) async-start(bf16[8,8,5632]{2,1,0:T(8,128)(2,1)} %bitcast.38), calls=%async_computation | async-start | bytes 1441792 | tf_op jit(solution)/shard_map/all_to_all | solution.py:332
  22.5 0.8 slice.24
  23.3 9.8 %collective-permute-start.4 = (bf16[8,2816]{1,0:T(8,128)(2,1)S(1)}, bf16[8,2816]{1,0:T(8,128)(2,1)S(1)}, u32[]{:S(2)}, u32[]{:S(2)}) collective-permute-start(bf16[8,2816]{1,0:T(8,128)(2,1)S(1)} %slice.24), channel_id=1, source_target_pairs={{0,1},{1,2},{2,3},{4,5},{5,6},{6,7},{8,9},{9,10},{10,11},{12,13},{... | collective-permute-start | bytes 135176 | tf_op jit(solution)/shard_map/ppermute | solution.py:19
  33.2 1.4 %multiply_convert_fusion.1 = (bf16[16,16,32]{2,1,0:T(8,128)(2,1)S(1)}, f32[16,16,32]{2,1,0:T(8,128)S(1)}) fusion(f32[64,256]{1,0:T(8,128)S(1)} %copy-done, s32[]{:T(128)S(6)} %select_n.38, s32[16,16]{1,0:T(8,128)} %param.14), kind=kOutput, calls=%fused_computation.3 | convolution fusion | flops 6324224 | bytes 82948 | tf_op jit(solution)/shard_map/bst,tc->bsc/dot_general | solution.py:281
  34.6 0.4 fusion.10
  35.5 1.7 %copy.15 = bf16[2,32,16,2,2,8]{5,4,3,2,1,0:T(2,128)(2,1)S(1)} copy(bf16[2,32,16,2,2,8]{1,4,5,2,3,0:T(2,128)(2,1)S(1)} %maximum_bitcast_fusion) | data formatting | bytes 131072 | tf_op jit(solution)/shard_map/transpose | solution.py:295
  37.2 0.6 copy-done.5
  37.8 4.5 %pulsar_spectra.1 = bf16[256,1408]{1,0:T(8,128)(2,1)} custom-call(bf16[8,2816]{1,0:T(8,128)(2,1)} %copy-done.5, bf16[8,45056]{1,0:T(8,128)(2,1)} %copy-done.3, f32[12,256]{1,0:T(8,128)} %taps_ref.3, bf16[256,512]{1,0:T(8,128)(2,1)} %constant.64.clone.table_ref), custom_call_target="tpu_custom_call" | custom-call | flops 600000000 | bytes 2000000 | tf_op jit(solution)/shard_map/pulsar_spectra/pallas_call | solution.py:127
  42.3 5.7 %all-to-all-start.1 = ((bf16[8,32,1408]{2,1,0:T(8,128)(2,1)}), bf16[8,32,1408]{2,1,0:T(8,128)(2,1)S(1)}, u32[]{:S(2)}, u32[]{:S(2)}) async-start(bf16[8,32,1408]{2,1,0:T(8,128)(2,1)} %bitcast.37), calls=%async_computation.1 | async-start | bytes 1441792 | tf_op jit(solution)/shard_map/all_to_all | solution.py:327
  48.0 7.0 %broadcast_multiply_fusion = bf16[2,32,16,2,2,8,32]{6,5,4,3,2,1,0:T(8,128)(2,1)} fusion(bf16[32,32]{1,0:T(8,128)(2,1)S(1)} %fusion.6, bf16[2,32,16,2,2,8]{5,4,3,2,1,0:T(2,128)(2,1)S(1)} %copy.15), kind=kLoop, calls=%fused_computation | loop fusion | flops 1048576 | bytes 2164736 | tf_op jit(solution)/shard_map/mul | solution.py:297
  55.0 12.4 %mul.47.weight_ref = bf16[1024,1024]{1,0:T(8,128)(2,1)} reshape(bf16[2,32,16,2,2,8,32]{6,5,4,3,2,1,0:T(8,128)(2,1)} %broadcast_multiply_fusion) | data formatting | bytes 4194304 | tf_op jit(solution)/shard_map/mul | solution.py:297
  67.4 2.0 %gram.1 = f32[64,64]{1,0:T(8,128)} custom-call(bf16[64,5632]{1,0:T(8,128)(2,1)} %bitcast.35), custom_call_target="tpu_custom_call" | custom-call | flops 50000000 | bytes 1000000 | tf_op jit(solution)/shard_map/gram/pallas_call | solution.py:270
  69.5 0.7 dynamic-slice_bitcast_fusion.2
  70.2 2.8 %collective-permute-start.1 = (f32[16,64]{1,0:T(8,128)S(1)}, f32[16,64]{1,0:T(8,128)S(1)}, u32[]{:S(2)}, u32[]{:S(2)}) collective-permute-start(f32[16,64]{1,0:T(8,128)S(1)} %get-tuple-element.8), channel_id=1, source_target_pairs={{0,1},{1,2},{2,3},{3,0},{4,5},{5,6},{6,7},{7,4},{8,9},{9,10},{10,1... | collective-permute-start | bytes 12296 | tf_op jit(solution)/shard_map/ppermute | solution.py:307
  73.0 1.9 %collective-permute-start.2 = (f32[16,64]{1,0:T(8,128)S(1)}, f32[16,64]{1,0:T(8,128)S(1)}, u32[]{:S(2)}, u32[]{:S(2)}) collective-permute-start(f32[16,64]{1,0:T(8,128)S(1)} %get-tuple-element.10), channel_id=1, source_target_pairs={{0,2},{1,3},{2,0},{3,1},{4,6},{5,7},{6,4},{7,5},{8,10},{9,11},{10,... | collective-permute-start | bytes 12296 | tf_op jit(solution)/shard_map/ppermute | solution.py:307
  74.9 0.9 %copy-done.2 = bf16[8,32,1408]{2,1,0:T(8,128)(2,1)} copy-done((bf16[8,32,1408]{2,1,0:T(8,128)(2,1)}, bf16[8,32,1408]{2,1,0:T(8,128)(2,1)S(1)}, u32[]{:S(2)}) %copy-start.2) | copy-done | bytes 720920
  75.8 4.8 %beam_former.1 = f32[512,176]{1,0:T(8,128)} custom-call(bf16[1024,1024]{1,0:T(8,128)(2,1)} %mul.47.weight_ref, bf16[256,1408]{1,0:T(8,128)(2,1)} %bitcast.36), custom_call_target="tpu_custom_call" | custom-call | flops 700000000 | bytes 4000000 | tf_op jit(solution)/shard_map/beam_former/pallas_call | solution.py:255
  80.6 0.7 fusion.8
  82.0 0.6 copy.16
  (23 shorter events, 1.1 us)
Async XLA Ops:
  0.6 32.5 %copy-start = (f32[64,256]{1,0:T(8,128)S(1)}, f32[64,256]{1,0:T(8,128)}, u32[]{:S(2)}) copy-start(f32[64,256]{1,0:T(8,128)} %param.13) | copy-start | bytes 196612
  2.1 4.2 %copy-start.3 = (bf16[8,45056]{1,0:T(8,128)(2,1)}, bf16[8,45056]{1,0:T(8,128)(2,1)S(1)}, u32[]{:S(2)}) copy-start(bf16[8,45056]{1,0:T(8,128)(2,1)S(1)} %reshape.132.own_ref) | copy-start | bytes 2162692
  2.1 4.2 %collective-permute-start = (bf16[8,45056]{1,0:T(8,128)(2,1)S(1)}, bf16[8,45056]{1,0:T(8,128)(2,1)S(1)}, u32[]{:S(2)}, u32[]{:S(2)}) collective-permute-start(bf16[8,45056]{1,0:T(8,128)(2,1)S(1)} %reshape.132.own_ref), channel_id=1, source_target_pairs={{0,1},{1,2},{2,3},{4,5},{5,6},{6,7},{8,9},{9,10},{10,11},{12,13},{... | collective-permute-start | bytes 2162696 | tf_op jit(solution)/shard_map/ppermute | solution.py:19
  6.3 0.9 %copy-start.4 = (bf16[8,45056]{1,0:T(8,128)(2,1)}, bf16[8,45056]{1,0:T(8,128)(2,1)S(1)}, u32[]{:S(2)}) copy-start(bf16[8,45056]{1,0:T(8,128)(2,1)S(1)} %collective-permute-done.history_ref) | copy-start | bytes 2162692
  15.9 26.4 %all-to-all-start = ((bf16[8,8,5632]{2,1,0:T(8,128)(2,1)}), bf16[8,8,5632]{2,1,0:T(8,128)(2,1)S(1)}, u32[]{:S(2)}, u32[]{:S(2)}) async-start(bf16[8,8,5632]{2,1,0:T(8,128)(2,1)} %bitcast.38), calls=%async_computation | async-start | bytes 1441792 | tf_op jit(solution)/shard_map/all_to_all | solution.py:332
  23.3 13.9 %collective-permute-start.4 = (bf16[8,2816]{1,0:T(8,128)(2,1)S(1)}, bf16[8,2816]{1,0:T(8,128)(2,1)S(1)}, u32[]{:S(2)}, u32[]{:S(2)}) collective-permute-start(bf16[8,2816]{1,0:T(8,128)(2,1)S(1)} %slice.24), channel_id=1, source_target_pairs={{0,1},{1,2},{2,3},{4,5},{5,6},{6,7},{8,9},{9,10},{10,11},{12,13},{... | collective-permute-start | bytes 135176 | tf_op jit(solution)/shard_map/ppermute | solution.py:19
  37.2 0.6 copy-start.5
  42.3 25.1 %copy-start.1 = (bf16[8,8,5632]{2,1,0:T(8,128)(2,1)}, bf16[8,8,5632]{2,1,0:T(8,128)(2,1)S(1)}, u32[]{:S(2)}) copy-start(bf16[8,8,5632]{2,1,0:T(8,128)(2,1)S(1)} %all-to-all-done) | copy-start | bytes 2162692
  42.3 32.6 %all-to-all-start.1 = ((bf16[8,32,1408]{2,1,0:T(8,128)(2,1)}), bf16[8,32,1408]{2,1,0:T(8,128)(2,1)S(1)}, u32[]{:S(2)}, u32[]{:S(2)}) async-start(bf16[8,32,1408]{2,1,0:T(8,128)(2,1)} %bitcast.37), calls=%async_computation.1 | async-start | bytes 1441792 | tf_op jit(solution)/shard_map/all_to_all | solution.py:327
  70.2 10.4 %collective-permute-start.1 = (f32[16,64]{1,0:T(8,128)S(1)}, f32[16,64]{1,0:T(8,128)S(1)}, u32[]{:S(2)}, u32[]{:S(2)}) collective-permute-start(f32[16,64]{1,0:T(8,128)S(1)} %get-tuple-element.8), channel_id=1, source_target_pairs={{0,1},{1,2},{2,3},{3,0},{4,5},{5,6},{6,7},{7,4},{8,9},{9,10},{10,1... | collective-permute-start | bytes 12296 | tf_op jit(solution)/shard_map/ppermute | solution.py:307
  73.0 7.6 %collective-permute-start.3 = (f32[16,64]{1,0:T(8,128)S(1)}, f32[16,64]{1,0:T(8,128)S(1)}, u32[]{:S(2)}, u32[]{:S(2)}) collective-permute-start(f32[16,64]{1,0:T(8,128)S(1)} %get-tuple-element.9), channel_id=1, source_target_pairs={{0,3},{1,0},{2,1},{3,2},{4,7},{5,4},{6,5},{7,6},{8,11},{9,8},{10,9... | collective-permute-start | bytes 12296 | tf_op jit(solution)/shard_map/ppermute | solution.py:307
  73.0 7.6 %collective-permute-start.2 = (f32[16,64]{1,0:T(8,128)S(1)}, f32[16,64]{1,0:T(8,128)S(1)}, u32[]{:S(2)}, u32[]{:S(2)}) collective-permute-start(f32[16,64]{1,0:T(8,128)S(1)} %get-tuple-element.10), channel_id=1, source_target_pairs={{0,2},{1,3},{2,0},{3,1},{4,6},{5,7},{6,4},{7,5},{8,10},{9,11},{10,... | collective-permute-start | bytes 12296 | tf_op jit(solution)/shard_map/ppermute | solution.py:307
  74.9 0.9 %copy-start.2 = (bf16[8,32,1408]{2,1,0:T(8,128)(2,1)}, bf16[8,32,1408]{2,1,0:T(8,128)(2,1)S(1)}, u32[]{:S(2)}) copy-start(bf16[8,32,1408]{2,1,0:T(8,128)(2,1)S(1)} %all-to-all-done.1) | copy-start | bytes 2162692

commit v2 on v1

--- a/solution.py
+++ b/solution.py
@@ -1,4 +1,3 @@
-import functools
 import math
 
 import jax
@@ -11,6 +10,7 @@
 
 LANES = 128
 GROUPS = 8
+VMEM_BYTES = 24 * 1024 * 1024
 
 
 def from_behind(array, axis, by):
@@ -132,7 +132,8 @@
             pltpu.VMEM((length // LANES, rows * frames, LANES), jnp.float32),
             pltpu.VMEM((rows * frames, 2 * length), jnp.bfloat16),
         ],
-        cost_estimate=pl.CostEstimate(flops=600000000, bytes_accessed=2000000, transcendentals=0),
+        cost_estimate=pl.CostEstimate(flops=5000000000, bytes_accessed=2000000, transcendentals=0),
+        compiler_params=pltpu.CompilerParams(vmem_limit_bytes=VMEM_BYTES),
         name="pulsar_spectra",
     )(history, own, taps, table)
 
@@ -222,41 +223,53 @@
             pltpu.VMEM((GROUPS, frames * height // GROUPS, 2 * LANES), jnp.bfloat16),
             pltpu.VMEM((GROUPS, frames * height // GROUPS, LANES), jnp.float32),
         ],
-        cost_estimate=pl.CostEstimate(flops=1000000000, bytes_accessed=4000000, transcendentals=0),
+        cost_estimate=pl.CostEstimate(flops=10000000000, bytes_accessed=4000000, transcendentals=0),
+        compiler_params=pltpu.CompilerParams(vmem_limit_bytes=VMEM_BYTES),
         name="correlator_spectra",
     )(history, own, taps, first, second, jnp.asarray(twist_cos), jnp.asarray(twist_sin))
 
 
 def beam_kernel(weight_ref, spec_ref, out_ref, stacked):
-    sources = spec_ref.shape[0]
-    depth = weight_ref.shape[1]
-    terms = depth // sources
+    groups, depth, _ = stacked.shape
+    members = depth // weight_ref.shape[2]
+    sources = spec_ref.shape[0] // (members * groups)
+    terms = weight_ref.shape[2] // sources
     width = spec_ref.shape[1] // terms
-    for i in range(terms):
-        stacked[i * sources : (i + 1) * sources, :] = spec_ref[:, i * width : (i + 1) * width]
-    height = weight_ref.shape[0] // 2
-    chunk = min(height, 128)
+    height = weight_ref.shape[1] // groups
     frames = width // 2
-
-    def form(step, carry):
-        at = pl.multiple_of(step * chunk, chunk)
-        real_part = dot(weight_ref[pl.ds(at, chunk), :], stacked[...])
-        imag_part = dot(weight_ref[pl.ds(height + at, chunk), :], stacked[...])
-        power = real_part * real_part + imag_part * imag_part
-        out_ref[pl.ds(at, chunk), :] = power[:, :frames] + power[:, frames:]
-        return carry
-
-    lax.fori_loop(0, height // chunk, form, 0)
-
-
-def beam_former(weights, spectra):
-    terms = weights.shape[1] // spectra.shape[0]
-    width = spectra.shape[1] // terms
+    for term in range(terms):
+        piece = spec_ref[:, term * width : (term + 1) * width]
+        for source in range(sources):
+            for group in range(groups):
+                start = (source * groups + group) * members
+                at = (term * sources + source) * members
+                stacked[group, at : at + members, :] = piece[start : start + members]
+    beams = height // members
+    spread = lax.broadcasted_iota(jnp.int32, (weight_ref.shape[2], depth), 1) // members
+    spread = (spread == lax.broadcasted_iota(jnp.int32, (weight_ref.shape[2], depth), 0)).astype(jnp.bfloat16)
+    same = lax.broadcasted_iota(jnp.int32, (height, depth), 0) // beams
+    same = same == lax.broadcasted_iota(jnp.int32, (height, depth), 1) % members
+    for group in range(groups):
+        power = None
+        for part in range(2):
+            rows = weight_ref[part, group * height : (group + 1) * height, :]
+            wide = jnp.where(same, dot(rows, spread), 0.0).astype(jnp.bfloat16)
+            field = dot(wide, stacked[group])
+            power = field * field if power is None else power + field * field
+        out_ref[group * height : (group + 1) * height, :] = power[:, :frames] + power[:, frames:]
+
+
+def beam_former(weights, spectra, channels):
+    _, height, terms = weights.shape
+    members = min(channels, 16)
+    groups = channels // members
+    width = spectra.shape[1] * spectra.shape[0] // (terms * channels)
     return pl.pallas_call(
         beam_kernel,
-        out_shape=jax.ShapeDtypeStruct((weights.shape[0] // 2, width // 2), jnp.float32),
-        scratch_shapes=[pltpu.VMEM((weights.shape[1], width), jnp.bfloat16)],
-        cost_estimate=pl.CostEstimate(flops=700000000, bytes_accessed=4000000, transcendentals=0),
+        out_shape=jax.ShapeDtypeStruct((height, width // 2), jnp.float32),
+        scratch_shapes=[pltpu.VMEM((groups, terms * members, width), jnp.bfloat16)],
+        compiler_params=pltpu.CompilerParams(vmem_limit_bytes=VMEM_BYTES),
+        cost_estimate=pl.CostEstimate(flops=4000000000, bytes_accessed=2000000, transcendentals=0),
         name="beam_former",
     )(weights, spectra)
 
@@ -270,7 +283,8 @@
     return pl.pallas_call(
         gram_kernel,
         out_shape=jax.ShapeDtypeStruct((rows, rows), jnp.float32),
-        cost_estimate=pl.CostEstimate(flops=50000000, bytes_accessed=1000000, transcendentals=0),
+        cost_estimate=pl.CostEstimate(flops=2000000000, bytes_accessed=1000000, transcendentals=0),
+        compiler_params=pltpu.CompilerParams(vmem_limit_bytes=VMEM_BYTES),
         name="gram",
     )(spectra)
 
@@ -286,15 +300,14 @@
     )
 
 
-def beam_matrix(weight_real, weight_imag, local_stations):
+def beam_rows(weight_real, weight_imag, local_stations):
     beams, stations, channels = weight_real.shape
     parts = jnp.stack(
         [jnp.stack([weight_real, -weight_imag], 0), jnp.stack([weight_imag, weight_real], 0)], 0
     )
     parts = parts.reshape(2, 2, beams, stations // local_stations, local_stations, channels)
-    parts = parts.transpose(0, 5, 2, 1, 4, 3)[..., None]
-    same = jnp.eye(channels, dtype=jnp.bfloat16).reshape(1, channels, 1, 1, 1, 1, channels)
-    return (parts * same).reshape(2 * channels * beams, 2 * stations * channels)
+    parts = parts.transpose(0, 5, 2, 1, 4, 3)
+    return parts.reshape(2, channels * beams, 2 * stations)
 
 
 def sum_over_grp(matrix):
@@ -334,8 +347,8 @@
         angle_table, lax.axis_index("stn") * owned_channels, owned_channels, 1
     )
     weight_real, weight_imag = station_weights(table_index, columns, station_total)
-    matrix = beam_matrix(weight_real, weight_imag, local_stations)
-    beam_power = beam_former(matrix, short_turned.reshape(owners * owned_channels, -1))
+    weights = beam_rows(weight_real, weight_imag, local_stations)
+    beam_power = beam_former(weights, short_turned.reshape(owners * owned_channels, -1), owned_channels)
     beam_power = beam_power.reshape(owned_channels, table_index.shape[0], -1)
     inner_depth = turned.shape[2]
     products = gram(turned.reshape(owners * rows, inner_depth))
@@ -355,6 +368,4 @@
 def solution(mesh):
     in_specs = (P(None, "stn", None, "grp"), P(), P(), P(), P())
     out_specs = (P("stn", "grp", None, None), P("stn", None, "grp"))
-    return jax.shard_map(
-        on_device, mesh=mesh, in_specs=in_specs, out_specs=out_specs, check_vma=False
-    )
+    return jax.shard_map(on_device, mesh=mesh, in_specs=in_specs, out_specs=out_specs, check_vma=False)

time: 83.5 us -> 63.5 us (0.76)
  the two profiles are of different devices: /device:TPU:0 before, /device:TPU:1 now
where the time goes in v2:
time: 63.5 us; the launch traced here: 63.1 us
  starting transfers between devices  21.8 us (34%)
  waiting for transfers between devices  21.4 us (34%)
  Pallas kernels  12.9 us (20%)
  local copies, waits for them, and re-layouts  4.56 us (7%)
  between operations  0.9 us (1%)
  other arithmetic  0.83 us (1%)
  matrix products  0.68 us (1%)
    ppermute x2, waiting for transfers between devices, from_behind(): return lax.ppermute(array, axis, pairs)  9.33 us
    ppermute x2, starting transfers between devices, from_behind(): return lax.ppermute(array, axis, pairs)  9.21 us
    all_to_all x1, waiting for transfers between devices, on_device(): lax.all_to_all(short, 'stn', split_axis=0, concat_axis=0, tiled=True)  9.17 us
    pallas_call x1, Pallas kernels, correlator_spectra(): pl.pallas_call(correlator_kernel, out_shape=jax.ShapeDtypeStruct((GROUPS...  7.08 us
    all_to_all x1, starting transfers between devices, on_device(): lax.all_to_all(spectra, 'stn', split_axis=0, concat_axis=0, tiled=True)  5.65 us
    all_to_all x1, starting transfers between devices, on_device(): lax.all_to_all(short, 'stn', split_axis=0, concat_axis=0, tiled=True)  3.54 us
    ppermute x3, starting transfers between devices, sum_over_grp(): lax.ppermute(away, 'grp', [(i, (i + by) % members) for i in range(members)])  3.39 us
    pallas_call x1, Pallas kernels, pulsar_spectra(): pl.pallas_call(pulsar_kernel, out_shape=jax.ShapeDtypeStruct((length, row...  3.29 us
  transfers between devices with their start and end apart: 7, of which 4 were waited for; matrix products, arithmetic and copies ran while one was open for 4% of the time, Pallas kernels for 9%

profile of v2, /device:TPU:1, one launch (start us, length us, event | category | flops | bytes accessed | tf_op | source)
XLA Modules:
  0.0 63.1 jit_solution(304336095380476006)
XLA Ops:
  0.7 1.5 %reshape.121.own_ref = bf16[8,45056]{1,0:T(8,128)(2,1)S(1)} reshape(bf16[2,2,2,45056]{3,2,1,0:T(2,128)(2,1)} %param.10) | data formatting | bytes 1441792 | tf_op jit(solution)/shard_map/reshape | solution.py:333
  2.2 4.5 %collective-permute-start = (bf16[8,45056]{1,0:T(8,128)(2,1)S(1)}, bf16[8,45056]{1,0:T(8,128)(2,1)S(1)}, u32[]{:S(2)}, u32[]{:S(2)}) collective-permute-start(bf16[8,45056]{1,0:T(8,128)(2,1)S(1)} %reshape.121.own_ref), channel_id=1, source_target_pairs={{0,1},{1,2},{2,3},{4,5},{5,6},{6,7},{8,9},{9,10},{10,11},{12,13},{... | collective-permute-start | bytes 2162696 | tf_op jit(solution)/shard_map/ppermute | solution.py:19
  6.7 8.2 %collective-permute-done.history_ref = bf16[8,45056]{1,0:T(8,128)(2,1)S(1)} collective-permute-done((bf16[8,45056]{1,0:T(8,128)(2,1)S(1)}, bf16[8,45056]{1,0:T(8,128)(2,1)S(1)}, u32[]{:S(2)}, u32[]{:S(2)}) %collective-permute-start) | collective-permute-done | bytes 720928 | tf_op jit(solution)/shard_map/ppermute | solution.py:19
  15.0 7.1 %correlator_spectra.1 = bf16[64,5632]{1,0:T(8,128)(2,1)} custom-call(bf16[8,45056]{1,0:T(8,128)(2,1)S(1)} %collective-permute-done.history_ref, bf16[8,45056]{1,0:T(8,128)(2,1)S(1)} %reshape.121.own_ref, f32[12,4096]{1,0:T(8,128)S(1)} %copy-done.1, bf16[512,256]{1,0:T(8,128)(2,1)S(1)} %copy-done.5, bf16[256,1024]{1,0:T(8,128)(2,1)S(1)} %copy-done.3, ...), custom_call_target="tpu_custom_call" | custom-call | flops 10000000000 | bytes 4000000 | tf_op jit(solution)/shard_map/correlator_spectra/pallas_call | solution.py:217
  22.0 5.6 %all-to-all-start = ((bf16[8,8,5632]{2,1,0:T(8,128)(2,1)}), bf16[8,8,5632]{2,1,0:T(8,128)(2,1)S(1)}, u32[]{:S(2)}, u32[]{:S(2)}) async-start(bf16[8,8,5632]{2,1,0:T(8,128)(2,1)} %bitcast), calls=%async_computation | async-start | bytes 1441792 | tf_op jit(solution)/shard_map/all_to_all | solution.py:345
  27.7 4.7 %collective-permute-start.4 = (bf16[8,2816]{1,0:T(8,128)(2,1)S(1)}, bf16[8,2816]{1,0:T(8,128)(2,1)S(1)}, u32[]{:S(2)}, u32[]{:S(2)}) collective-permute-start(bf16[8,2816]{1,0:T(8,128)(2,1)S(1)} %slice.24), channel_id=1, source_target_pairs={{0,1},{1,2},{2,3},{4,5},{5,6},{6,7},{8,9},{9,10},{10,11},{12,13},{... | collective-permute-start | bytes 135176 | tf_op jit(solution)/shard_map/ppermute | solution.py:19
  32.4 1.1 %collective-permute-done.4.history_ref = bf16[8,2816]{1,0:T(8,128)(2,1)S(1)} collective-permute-done((bf16[8,2816]{1,0:T(8,128)(2,1)S(1)}, bf16[8,2816]{1,0:T(8,128)(2,1)S(1)}, u32[]{:S(2)}, u32[]{:S(2)}) %collective-permute-start.4) | collective-permute-done | bytes 45088 | tf_op jit(solution)/shard_map/ppermute | solution.py:19
  33.5 3.3 %pulsar_spectra.1 = bf16[256,1408]{1,0:T(8,128)(2,1)} custom-call(bf16[8,2816]{1,0:T(8,128)(2,1)S(1)} %collective-permute-done.4.history_ref, bf16[8,45056]{1,0:T(8,128)(2,1)S(1)} %reshape.121.own_ref, f32[12,256]{1,0:T(8,128)S(1)} %copy-done.2, bf16[256,512]{1,0:T(8,128)(2,1)S(1)} %copy-done.4), custom_call_target="tpu_custom_call" | custom-call | flops 5000000000 | bytes 2000000 | tf_op jit(solution)/shard_map/pulsar_spectra/pallas_call | solution.py:127
  36.8 2.9 %all-to-all-done = bf16[8,8,5632]{2,1,0:T(8,128)(2,1)S(1)} async-done(((bf16[8,8,5632]{2,1,0:T(8,128)(2,1)}), bf16[8,8,5632]{2,1,0:T(8,128)(2,1)S(1)}, u32[]{:S(2)}, u32[]{:S(2)}) %all-to-all-start) | async-done | bytes 720928 | tf_op jit(solution)/shard_map/all_to_all | solution.py:345
  39.8 3.5 %all-to-all-start.1 = ((bf16[8,32,1408]{2,1,0:T(8,128)(2,1)}), bf16[8,32,1408]{2,1,0:T(8,128)(2,1)S(1)}, u32[]{:S(2)}, u32[]{:S(2)}) async-start(bf16[8,32,1408]{2,1,0:T(8,128)(2,1)} %bitcast.12), calls=%async_computation.1 | async-start | bytes 1441792 | tf_op jit(solution)/shard_map/all_to_all | solution.py:340
  43.4 0.7 %copy-done.8 = s32[16,16]{1,0:T(8,128)S(1)} copy-done((s32[16,16]{1,0:T(8,128)S(1)}, s32[16,16]{1,0:T(8,128)}, u32[]{:S(2)}) %copy-start.8) | copy-done | bytes 1048
  44.0 0.7 %multiply_convert_fusion.1 = (bf16[16,16,32]{2,1,0:T(8,128)(2,1)S(1)}, f32[16,16,32]{2,1,0:T(8,128)S(1)}) fusion(f32[64,256]{1,0:T(8,128)S(1)} %copy-done, s32[]{:T(128)S(6)} %select_n.38, s32[16,16]{1,0:T(8,128)S(1)} %copy-done.8), kind=kOutput, calls=%fused_computation.2 | convolution fusion | flops 6324224 | bytes 90116 | tf_op jit(solution)/shard_map/bst,tc->bsc/dot_general | solution.py:295
  44.9 0.4 fusion.9
  45.5 0.1 copy.19
  45.6 0.1 maximum_bitcast_fusion
  45.8 0.8 %reshape.125 = bf16[2,512,32]{1,2,0:T(8,128)(2,1)S(1)} reshape(bf16[2,32,16,2,2,8]{2,1,5,4,3,0:T(8,128)(2,1)S(1)} %maximum_bitcast_fusion) | data formatting | bytes 131072 | tf_op jit(solution)/shard_map/reshape | solution.py:310
  46.5 0.2 copy.22.weight_ref
  46.7 0.3 gram.1
  47.1 3.3 %collective-permute-start.2 = (f32[16,64]{1,0:T(8,128)S(1)}, f32[16,64]{1,0:T(8,128)S(1)}, u32[]{:S(2)}, u32[]{:S(2)}) collective-permute-start(f32[16,64]{1,0:T(8,128)S(1)} %get-tuple-element.10), channel_id=1, source_target_pairs={{0,2},{1,3},{2,0},{3,1},{4,6},{5,7},{6,4},{7,5},{8,10},{9,11},{10,... | collective-permute-start | bytes 12296 | tf_op jit(solution)/shard_map/ppermute | solution.py:320
  50.5 9.2 %all-to-all-done.1 = bf16[8,32,1408]{2,1,0:T(8,128)(2,1)S(1)} async-done(((bf16[8,32,1408]{2,1,0:T(8,128)(2,1)}), bf16[8,32,1408]{2,1,0:T(8,128)(2,1)S(1)}, u32[]{:S(2)}, u32[]{:S(2)}) %all-to-all-start.1) | async-done | bytes 720928 | tf_op jit(solution)/shard_map/all_to_all | solution.py:340
  59.6 2.2 %beam_former.1 = f32[512,176]{1,0:T(8,128)} custom-call(bf16[2,512,32]{2,1,0:T(8,128)(2,1)S(1)} %copy.22.weight_ref, bf16[256,1408]{1,0:T(8,128)(2,1)S(1)} %bitcast.37), custom_call_target="tpu_custom_call" | custom-call | flops 4000000000 | bytes 2000000 | tf_op jit(solution)/shard_map/beam_former/pallas_call | solution.py:267
  61.8 0.2 reshape.124
  62.1 0.2 fusion.3
  62.5 0.6 copy.23
  (30 shorter events, 0.6 us)
Async XLA Ops:
  0.6 42.7 %copy-start = (f32[64,256]{1,0:T(8,128)S(1)}, f32[64,256]{1,0:T(8,128)}, u32[]{:S(2)}) copy-start(f32[64,256]{1,0:T(8,128)} %param.13) | copy-start | bytes 196612
  0.6 14.3 %copy-start.3 = (bf16[256,1024]{1,0:T(8,128)(2,1)S(1)}, bf16[256,1024]{1,0:T(8,128)(2,1)}, u32[]{:S(2)}) copy-start(bf16[256,1024]{1,0:T(8,128)(2,1)} %constant.66.clone.second_ref) | copy-start | bytes 1572868
  0.7 14.3 %copy-start.5 = (bf16[512,256]{1,0:T(8,128)(2,1)S(1)}, bf16[512,256]{1,0:T(8,128)(2,1)}, u32[]{:S(2)}) copy-start(bf16[512,256]{1,0:T(8,128)(2,1)} %constant.65.clone.first_ref) | copy-start | bytes 786436
  0.7 14.3 %copy-start.6 = (f32[256,128]{1,0:T(8,128)S(1)}, f32[256,128]{1,0:T(8,128)}, u32[]{:S(2)}) copy-start(f32[256,128]{1,0:T(8,128)} %constant.67.clone.cos_ref) | copy-start | bytes 393220
  0.7 14.3 %copy-start.7 = (f32[256,128]{1,0:T(8,128)S(1)}, f32[256,128]{1,0:T(8,128)}, u32[]{:S(2)}) copy-start(f32[256,128]{1,0:T(8,128)} %constant.68.clone.sin_ref) | copy-start | bytes 393220
  0.7 14.3 %copy-start.1 = (f32[12,4096]{1,0:T(8,128)S(1)}, f32[12,4096]{1,0:T(8,128)}, u32[]{:S(2)}) copy-start(f32[12,4096]{1,0:T(8,128)} %taps_ref.2) | copy-start | bytes 589828
  2.2 12.7 %collective-permute-start = (bf16[8,45056]{1,0:T(8,128)(2,1)S(1)}, bf16[8,45056]{1,0:T(8,128)(2,1)S(1)}, u32[]{:S(2)}, u32[]{:S(2)}) collective-permute-start(bf16[8,45056]{1,0:T(8,128)(2,1)S(1)} %reshape.121.own_ref), channel_id=1, source_target_pairs={{0,1},{1,2},{2,3},{4,5},{5,6},{6,7},{8,9},{9,10},{10,11},{12,13},{... | collective-permute-start | bytes 2162696 | tf_op jit(solution)/shard_map/ppermute | solution.py:19
  22.0 11.5 %copy-start.4 = (bf16[256,512]{1,0:T(8,128)(2,1)S(1)}, bf16[256,512]{1,0:T(8,128)(2,1)}, u32[]{:S(2)}) copy-start(bf16[256,512]{1,0:T(8,128)(2,1)} %constant.64.clone.table_ref) | copy-start | bytes 786436
  22.0 17.7 %all-to-all-start = ((bf16[8,8,5632]{2,1,0:T(8,128)(2,1)}), bf16[8,8,5632]{2,1,0:T(8,128)(2,1)S(1)}, u32[]{:S(2)}, u32[]{:S(2)}) async-start(bf16[8,8,5632]{2,1,0:T(8,128)(2,1)} %bitcast), calls=%async_computation | async-start | bytes 1441792 | tf_op jit(solution)/shard_map/all_to_all | solution.py:345
  27.7 5.8 %copy-start.2 = (f32[12,256]{1,0:T(8,128)S(1)}, f32[12,256]{1,0:T(8,128)}, u32[]{:S(2)}) copy-start(f32[12,256]{1,0:T(8,128)} %taps_ref.3) | copy-start | bytes 36868
  27.7 5.8 %collective-permute-start.4 = (bf16[8,2816]{1,0:T(8,128)(2,1)S(1)}, bf16[8,2816]{1,0:T(8,128)(2,1)S(1)}, u32[]{:S(2)}, u32[]{:S(2)}) collective-permute-start(bf16[8,2816]{1,0:T(8,128)(2,1)S(1)} %slice.24), channel_id=1, source_target_pairs={{0,1},{1,2},{2,3},{4,5},{5,6},{6,7},{8,9},{9,10},{10,11},{12,13},{... | collective-permute-start | bytes 135176 | tf_op jit(solution)/shard_map/ppermute | solution.py:19
  39.8 19.9 %all-to-all-start.1 = ((bf16[8,32,1408]{2,1,0:T(8,128)(2,1)}), bf16[8,32,1408]{2,1,0:T(8,128)(2,1)S(1)}, u32[]{:S(2)}, u32[]{:S(2)}) async-start(bf16[8,32,1408]{2,1,0:T(8,128)(2,1)} %bitcast.12), calls=%async_computation.1 | async-start | bytes 1441792 | tf_op jit(solution)/shard_map/all_to_all | solution.py:340
  43.3 0.7 %copy-start.8 = (s32[16,16]{1,0:T(8,128)S(1)}, s32[16,16]{1,0:T(8,128)}, u32[]{:S(2)}) copy-start(s32[16,16]{1,0:T(8,128)} %param.14) | copy-start | bytes 3076
  47.1 14.7 %collective-permute-start.3 = (f32[16,64]{1,0:T(8,128)S(1)}, f32[16,64]{1,0:T(8,128)S(1)}, u32[]{:S(2)}, u32[]{:S(2)}) collective-permute-start(f32[16,64]{1,0:T(8,128)S(1)} %get-tuple-element.9), channel_id=1, source_target_pairs={{0,3},{1,0},{2,1},{3,2},{4,7},{5,4},{6,5},{7,6},{8,11},{9,8},{10,9... | collective-permute-start | bytes 12296 | tf_op jit(solution)/shard_map/ppermute | solution.py:320
  47.1 14.7 %collective-permute-start.2 = (f32[16,64]{1,0:T(8,128)S(1)}, f32[16,64]{1,0:T(8,128)S(1)}, u32[]{:S(2)}, u32[]{:S(2)}) collective-permute-start(f32[16,64]{1,0:T(8,128)S(1)} %get-tuple-element.10), channel_id=1, source_target_pairs={{0,2},{1,3},{2,0},{3,1},{4,6},{5,7},{6,4},{7,5},{8,10},{9,11},{10,... | collective-permute-start | bytes 12296 | tf_op jit(solution)/shard_map/ppermute | solution.py:320
  50.4 11.4 %collective-permute-start.1 = (f32[16,64]{1,0:T(8,128)S(1)}, f32[16,64]{1,0:T(8,128)S(1)}, u32[]{:S(2)}, u32[]{:S(2)}) collective-permute-start(f32[16,64]{1,0:T(8,128)S(1)} %get-tuple-element.8), channel_id=1, source_target_pairs={{0,1},{1,2},{2,3},{3,0},{4,5},{5,6},{6,7},{7,4},{8,9},{9,10},{10,1... | collective-permute-start | bytes 12296 | tf_op jit(solution)/shard_map/ppermute | solution.py:320

commit v3 on v2

--- a/solution.py
+++ b/solution.py
@@ -1,3 +1,4 @@
+import functools
 import math
 
 import jax
@@ -10,6 +11,8 @@
 
 LANES = 128
 GROUPS = 8
+CROSS = (6, 7, 4, 5)
+NEAR = (2, 3, 1)
 VMEM_BYTES = 24 * 1024 * 1024
 
 
@@ -64,7 +67,8 @@
     )
 
 
-def pulsar_kernel(history_ref, own_ref, taps_ref, table_ref, out_ref, wide, summed, stacked):
+def pulsar_kernel(me_ref, history_ref, own_ref, taps_ref, table_ref, *refs):
+    out_refs, (wide, summed, stacked, turned) = refs[:GROUPS], refs[GROUPS:]
     rows = own_ref.shape[0]
     taps, length = taps_ref.shape
     parts = length // LANES
@@ -115,10 +119,20 @@
         return carry
 
     lax.fori_loop(0, half // 64, stack, 0)
-    out_ref[...] = dot_rows(table_ref[...], stacked[...]).astype(jnp.bfloat16)
-
-
-def pulsar_spectra(history, own, taps):
+    share = length // GROUPS
+    for slot in range(GROUPS):
+        at = pl.multiple_of((slot ^ me_ref[0]) * share, share)
+        turned[slot * share : (slot + 1) * share, :] = table_ref[pl.ds(at, share), :]
+    spectra = dot_rows(turned[...], stacked[...]).astype(jnp.bfloat16)
+    for slot in range(GROUPS):
+        out_refs[slot][...] = spectra[slot * share : (slot + 1) * share]
+
+
+def on_chip(count):
+    return [pl.BlockSpec(memory_space=pltpu.SMEM)] + [pl.BlockSpec(memory_space=pltpu.VMEM)] * count
+
+
+def pulsar_spectra(me, history, own, taps):
     rows, samples = own.shape
     length = taps.shape[1]
     frames = samples // length
@@ -126,19 +140,22 @@
     blocks = (history.shape[1] + samples) // LANES
     return pl.pallas_call(
         pulsar_kernel,
-        out_shape=jax.ShapeDtypeStruct((length, rows * frames), jnp.bfloat16),
+        out_shape=[jax.ShapeDtypeStruct((length // GROUPS, rows * frames), jnp.bfloat16)] * GROUPS,
+        in_specs=on_chip(4),
         scratch_shapes=[
             pltpu.VMEM((blocks, rows, LANES), jnp.float32),
             pltpu.VMEM((length // LANES, rows * frames, LANES), jnp.float32),
             pltpu.VMEM((rows * frames, 2 * length), jnp.bfloat16),
+            pltpu.VMEM((length, 2 * length), jnp.bfloat16),
         ],
         cost_estimate=pl.CostEstimate(flops=5000000000, bytes_accessed=2000000, transcendentals=0),
         compiler_params=pltpu.CompilerParams(vmem_limit_bytes=VMEM_BYTES),
         name="pulsar_spectra",
-    )(history, own, taps, table)
-
-
-def correlator_kernel(history_ref, own_ref, taps_ref, first_ref, second_ref, cos_ref, sin_ref, out_ref, wide, summed, twisted, mixed):
+    )(me, history, own, taps, table)
+
+
+def correlator_kernel(me_ref, history_ref, own_ref, taps_ref, first_ref, second_ref, cos_ref, sin_ref, *refs):
+    out_refs, (wide, summed, twisted, mixed) = refs[:GROUPS], refs[GROUPS:]
     rows = own_ref.shape[0]
     taps, length = taps_ref.shape
     blocks = length // LANES
@@ -189,6 +206,7 @@
     for i in range(GROUPS):
         mixed[i] = dot(twisted[i], second_ref[:, i * LANES : (i + 1) * LANES])
     group = lax.broadcasted_iota(jnp.int32, (rows, LANES), 1) // (LANES // GROUPS)
+    swap = {bit: jnp.full((rows, LANES), me_ref[0] & bit, jnp.int32) != 0 for bit in (1, 2, 4)}
 
     def gather(step, carry):
         at = pl.multiple_of(step * rows, rows)
@@ -196,15 +214,19 @@
         for bit in (1, 2, 4):
             pick = (group & bit) != 0
             tiles = [jnp.where(pick, tiles[(i + bit) % GROUPS], tiles[i]) for i in range(GROUPS)]
+        tiles = [tiles[-d % GROUPS] for d in range(GROUPS)]
+        for bit in (1, 2, 4):
+            pick = swap[bit]
+            tiles = [jnp.where(pick, tiles[d ^ bit], tiles[d]) for d in range(GROUPS)]
         lane = pl.multiple_of(step * LANES, LANES)
-        for d in range(GROUPS):
-            out_ref[d * rows : (d + 1) * rows, pl.ds(lane, LANES)] = tiles[-d % GROUPS].astype(jnp.bfloat16)
+        for slot in range(GROUPS):
+            out_refs[slot][:, pl.ds(lane, LANES)] = tiles[slot].astype(jnp.bfloat16)
         return carry
 
     lax.fori_loop(0, frames * blocks // GROUPS, gather, 0)
 
 
-def correlator_spectra(history, own, taps):
+def correlator_spectra(me, history, own, taps):
     rows, samples = own.shape
     length = taps.shape[1]
     frames = samples // length
@@ -216,7 +238,8 @@
     tiles = frames * blocks // GROUPS
     return pl.pallas_call(
         correlator_kernel,
-        out_shape=jax.ShapeDtypeStruct((GROUPS * rows, tiles * LANES), jnp.bfloat16),
+        out_shape=[jax.ShapeDtypeStruct((rows, tiles * LANES), jnp.bfloat16)] * GROUPS,
+        in_specs=on_chip(7),
         scratch_shapes=[
             pltpu.VMEM(((frames + taps.shape[0] - 1) * blocks, rows, LANES), jnp.float32),
             pltpu.VMEM((frames, height, LANES), jnp.float32),
@@ -226,24 +249,28 @@
         cost_estimate=pl.CostEstimate(flops=10000000000, bytes_accessed=4000000, transcendentals=0),
         compiler_params=pltpu.CompilerParams(vmem_limit_bytes=VMEM_BYTES),
         name="correlator_spectra",
-    )(history, own, taps, first, second, jnp.asarray(twist_cos), jnp.asarray(twist_sin))
-
-
-def beam_kernel(weight_ref, spec_ref, out_ref, stacked):
-    groups, depth, _ = stacked.shape
+    )(me, history, own, taps, first, second, jnp.asarray(twist_cos), jnp.asarray(twist_sin))
+
+
+def beam_kernel(me_ref, weight_ref, *refs):
+    spec_refs, (out_ref, stacked) = refs[:GROUPS], refs[GROUPS:]
+    groups, depth, width = stacked.shape
     members = depth // weight_ref.shape[2]
-    sources = spec_ref.shape[0] // (members * groups)
-    terms = weight_ref.shape[2] // sources
-    width = spec_ref.shape[1] // terms
+    sources = spec_refs[0].shape[0] // (members * groups)
+    terms = spec_refs[0].shape[1] // width
     height = weight_ref.shape[1] // groups
     frames = width // 2
     for term in range(terms):
-        piece = spec_ref[:, term * width : (term + 1) * width]
-        for source in range(sources):
-            for group in range(groups):
-                start = (source * groups + group) * members
-                at = (term * sources + source) * members
-                stacked[group, at : at + members, :] = piece[start : start + members]
+        for slot in range(GROUPS):
+            piece = spec_refs[slot][:, term * width : (term + 1) * width]
+            for source in range(sources):
+                for group in range(groups):
+                    start = (source * groups + group) * members
+                    at = ((term * GROUPS + slot) * sources + source) * members
+                    if members % 8 == 0:
+                        place = (term * GROUPS + (slot ^ me_ref[0])) * sources + source
+                        at = pl.multiple_of(place * members, members)
+                    stacked[group, pl.ds(at, members), :] = piece[start : start + members]
     beams = height // members
     spread = lax.broadcasted_iota(jnp.int32, (weight_ref.shape[2], depth), 1) // members
     spread = (spread == lax.broadcasted_iota(jnp.int32, (weight_ref.shape[2], depth), 0)).astype(jnp.bfloat16)
@@ -259,34 +286,75 @@
         out_ref[group * height : (group + 1) * height, :] = power[:, :frames] + power[:, frames:]
 
 
-def beam_former(weights, spectra, channels):
+def beam_former(me, weights, spectra, channels):
     _, height, terms = weights.shape
     members = min(channels, 16)
     groups = channels // members
-    width = spectra.shape[1] * spectra.shape[0] // (terms * channels)
+    width = GROUPS * spectra[0].shape[1] * spectra[0].shape[0] // (terms * channels)
     return pl.pallas_call(
         beam_kernel,
         out_shape=jax.ShapeDtypeStruct((height, width // 2), jnp.float32),
+        in_specs=on_chip(1 + GROUPS),
         scratch_shapes=[pltpu.VMEM((groups, terms * members, width), jnp.bfloat16)],
         compiler_params=pltpu.CompilerParams(vmem_limit_bytes=VMEM_BYTES),
         cost_estimate=pl.CostEstimate(flops=4000000000, bytes_accessed=2000000, transcendentals=0),
         name="beam_former",
-    )(weights, spectra)
-
-
-def gram_kernel(spec_ref, out_ref):
-    out_ref[...] = dot_rows(spec_ref[...], spec_ref[...])
+    )(me, weights, *spectra)
+
+
+def gram_kernel(*refs):
+    spectra = jnp.concatenate([ref[...] for ref in refs[:GROUPS]], 0)
+    refs[GROUPS][...] = dot_rows(spectra, spectra)
 
 
 def gram(spectra):
-    rows = spectra.shape[0]
+    rows = GROUPS * spectra[0].shape[0]
     return pl.pallas_call(
         gram_kernel,
         out_shape=jax.ShapeDtypeStruct((rows, rows), jnp.float32),
+        compiler_params=pltpu.CompilerParams(vmem_limit_bytes=VMEM_BYTES),
         cost_estimate=pl.CostEstimate(flops=2000000000, bytes_accessed=1000000, transcendentals=0),
+        name="gram",
+    )(*spectra)
+
+
+def finish_kernel(pairs, scale, me_ref, *refs):
+    out_ref = refs[-1]
+    total = refs[0][...]
+    for ref in refs[1:-1]:
+        total = total + ref[...]
+    rows, columns = total.shape
+    held = rows // (2 * pairs)
+    signals = columns // 2
+    at = lax.broadcasted_iota(jnp.int32, (columns, signals), 0)
+    to = lax.broadcasted_iota(jnp.int32, (columns, signals), 1)
+    source = (at // (2 * pairs)) ^ me_ref[0]
+    wanted = source * pairs + at % pairs == to
+    part = at // pairs % 2
+    halves = []
+    for value in (0, 1):
+        pick = jnp.where(wanted & (part == value), scale, 0.0).astype(jnp.float32)
+        halves.append(
+            jnp.dot(total, pick, precision=lax.Precision.HIGHEST, preferred_element_type=jnp.float32)
+        )
+    for slot in range(held):
+        first = slot * 2 * pairs
+        real = slice(first, first + pairs)
+        imag = slice(first + pairs, first + 2 * pairs)
+        row = (slot ^ (me_ref[0] & (held - 1))) * pairs
+        out_ref[0, pl.ds(row, pairs), 0, :] = halves[0][real] + halves[1][imag]
+        out_ref[0, pl.ds(row, pairs), 1, :] = halves[0][imag] - halves[1][real]
+
+
+def finish(me, blocks, pairs, scale):
+    rows, columns = blocks[0].shape
+    return pl.pallas_call(
+        functools.partial(finish_kernel, pairs, scale),
+        out_shape=jax.ShapeDtypeStruct((1, rows // 2, 2, columns // 2), jnp.float32),
+        in_specs=on_chip(len(blocks)),
         compiler_params=pltpu.CompilerParams(vmem_limit_bytes=VMEM_BYTES),
-        name="gram",
-    )(spectra)
+        name="finish",
+    )(me, *blocks)
 
 
 def station_weights(index_rows, columns, station_total):
@@ -310,15 +378,35 @@
     return parts.reshape(2, channels * beams, 2 * stations)
 
 
-def sum_over_grp(matrix):
+def exchange(slots):
+    turned = list(slots)
+    for k in CROSS + NEAR:
+        turned[k] = lax.ppermute(slots[k], "stn", [(i, i ^ k) for i in range(GROUPS)])
+    return turned
+
+
+def exchange_all(slots, owners):
+    rows, columns = slots[0].shape
+    whole = jnp.concatenate(slots, 0).reshape(owners, GROUPS * rows // owners, columns)
+    whole = lax.all_to_all(whole, "stn", split_axis=0, concat_axis=0, tiled=True)
+    whole = whole.reshape(GROUPS, rows, columns)
+    return [whole[k] for k in range(GROUPS)]
+
+
+def shares_of_grp(me, products):
     members = lax.axis_size("grp")
-    me = lax.axis_index("grp")
-    blocks = matrix.reshape(members, matrix.shape[0] // members, matrix.shape[1])
-    total = lax.dynamic_index_in_dim(blocks, me, 0, keepdims=False)
-    for by in range(1, members):
-        away = lax.dynamic_index_in_dim(blocks, (me + by) % members, 0, keepdims=False)
-        total = total + lax.ppermute(away, "grp", [(i, (i + by) % members) for i in range(members)])
-    return total
+    here = lax.axis_index("grp")
+    rows = products.shape[0] // members
+    held = rows // (products.shape[0] // GROUPS) if rows * GROUPS > products.shape[0] else 1
+    blocks = products.reshape(members, rows, products.shape[1])
+    terms = []
+    for by in range(members):
+        block = ((here + by) % members) ^ (me // held)
+        block = lax.dynamic_index_in_dim(blocks, block, 0, keepdims=False)
+        if by:
+            block = lax.ppermute(block, "grp", [(i, (i + by) % members) for i in range(members)])
+        terms.append(block)
+    return terms
 
 
 def on_device(voltages, corr_taps, beam_taps, angle_table, table_index):
@@ -330,38 +418,38 @@
     station_total = local_stations * owners
     pairs = local_stations * polarizations
     rows = 2 * pairs
+    direct = owners == GROUPS and short_length // owners % 8 == 0
+    me = lax.axis_index("stn") if direct else jnp.int32(0)
+    me_array = jnp.reshape(me, (1,)).astype(jnp.int32)
     own = voltages.reshape(rows, samples)
     short_past = (tap_count - 1) * short_length
     near = from_behind(own[:, samples - short_past :], "grp", 1)
     past = from_behind(own[:, samples - (tap_count - 1) * length :], "grp", 1)
-    short = pulsar_spectra(near, own, beam_taps)
+    short = pulsar_spectra(me_array, near, own, beam_taps)
     owned_channels = short_length // owners
-    short = short.reshape(owners, owned_channels, short.shape[1])
-    short_turned = lax.all_to_all(short, "stn", split_axis=0, concat_axis=0, tiled=True)
-    spectra = correlator_spectra(past, own, corr_taps)
-    subs = owners // GROUPS
-    spectra = spectra.reshape(GROUPS, rows, -1, subs, LANES // GROUPS // subs)
-    spectra = spectra.transpose(0, 3, 1, 2, 4).reshape(owners, rows, -1)
-    turned = lax.all_to_all(spectra, "stn", split_axis=0, concat_axis=0, tiled=True)
+    short = exchange(short) if direct else exchange_all(short, owners)
+    spectra = correlator_spectra(me_array, past, own, corr_taps)
+    if direct:
+        turned = exchange(spectra)
+    else:
+        subs = owners // GROUPS
+        spectra = [
+            slot.reshape(rows, -1, subs, LANES // GROUPS // subs).transpose(2, 0, 1, 3).reshape(subs * rows, -1)
+            for slot in spectra
+        ]
+        turned = exchange_all(spectra, owners)
     columns = lax.dynamic_slice_in_dim(
         angle_table, lax.axis_index("stn") * owned_channels, owned_channels, 1
     )
     weight_real, weight_imag = station_weights(table_index, columns, station_total)
     weights = beam_rows(weight_real, weight_imag, local_stations)
-    beam_power = beam_former(weights, short_turned.reshape(owners * owned_channels, -1), owned_channels)
+    beam_power = beam_former(me_array, weights, short, owned_channels)
     beam_power = beam_power.reshape(owned_channels, table_index.shape[0], -1)
-    inner_depth = turned.shape[2]
-    products = gram(turned.reshape(owners * rows, inner_depth))
-    summed = sum_over_grp(products)
-    held = owners // lax.axis_size("grp")
-    summed = summed.reshape(held, 2, pairs, owners, 2, pairs)
-    real_part = summed[:, 0, :, :, 0] + summed[:, 1, :, :, 1]
-    imag_part = summed[:, 1, :, :, 0] - summed[:, 0, :, :, 1]
-    signals = owners * pairs
-    visibility = jnp.stack(
-        [real_part.reshape(held * pairs, signals), imag_part.reshape(held * pairs, signals)], 1
-    )
-    visibility = (visibility * (1.0 / math.sqrt(inner_depth * lax.axis_size("grp"))))[None]
+    inner_depth = samples // length * (length // owners)
+    products = gram(turned)
+    terms = shares_of_grp(me, products)
+    scale = 1.0 / math.sqrt(inner_depth * lax.axis_size("grp"))
+    visibility = finish(me_array, terms, pairs, scale)
     return (visibility, beam_power)
 
 

time: 63.5 us -> 63.4 us (level)
  the two profiles are of different devices: /device:TPU:1 before, /device:TPU:0 now
where the time goes in v3:
time: 63.4 us; the launch traced here: 62.3 us
  starting transfers between devices  37.8 us (60%)
  Pallas kernels  12.2 us (19%)
  local copies, waits for them, and re-layouts  5.37 us (8%)
  waiting for transfers between devices  4.68 us (7%)
  between operations  1 us (2%)
  matrix products  0.69 us (1%)
    ppermute x14, starting transfers between devices, exchange(): lax.ppermute(slots[k], 'stn', [(i, i ^ k) for i in range(GROUPS)])  28.2 us
    ppermute x2, starting transfers between devices, from_behind(): return lax.ppermute(array, axis, pairs)  7.06 us
    pallas_call x1, Pallas kernels, correlator_spectra(): pl.pallas_call(correlator_kernel, out_shape=[jax.ShapeDtypeStruct((rows,...  6.36 us
    ppermute x14, waiting for transfers between devices, exchange(): lax.ppermute(slots[k], 'stn', [(i, i ^ k) for i in range(GROUPS)])  4.67 us
    ppermute x3, starting transfers between devices, shares_of_grp(): lax.ppermute(block, 'grp', [(i, (i + by) % members) for i in range(member...  2.55 us
    pallas_call x1, Pallas kernels, pulsar_spectra(): pl.pallas_call(pulsar_kernel, out_shape=[jax.ShapeDtypeStruct((length //...  2.42 us
    pallas_call x1, Pallas kernels, beam_former(): pl.pallas_call(beam_kernel, out_shape=jax.ShapeDtypeStruct((height, width...  2.29 us
    another operation x2, local copies, waits for them, and re-layouts, beam_rows(): jnp.stack([weight_real, -weight_imag], 0)  1.55 us
  transfers between devices with their start and end apart: 19, of which 2 were waited for; matrix products, arithmetic and copies ran while one was open for 7% of the time, Pallas kernels for 18%

profile of v3, /device:TPU:0, one launch (start us, length us, event | category | flops | bytes accessed | tf_op | source)
XLA Modules:
  0.0 62.3 jit_solution(7435912740446133145)
XLA Ops:
  0.7 1.4 %reshape.34.own_ref = bf16[8,45056]{1,0:T(8,128)(2,1)S(1)} reshape(bf16[2,2,2,45056]{3,2,1,0:T(2,128)(2,1)} %param.10) | data formatting | bytes 1441792 | tf_op jit(solution)/shard_map/reshape | solution.py:424
  2.1 2.4 %collective-permute-start = (bf16[8,45056]{1,0:T(8,128)(2,1)S(1)}, bf16[8,45056]{1,0:T(8,128)(2,1)S(1)}, u32[]{:S(2)}, u32[]{:S(2)}) collective-permute-start(bf16[8,45056]{1,0:T(8,128)(2,1)S(1)} %reshape.34.own_ref), channel_id=1, source_target_pairs={{0,1},{1,2},{2,3},{4,5},{5,6},{6,7},{8,9},{9,10},{10,11},{12,13},{... | collective-permute-start | bytes 2162696 | tf_op jit(solution)/shard_map/ppermute | solution.py:22
  4.6 4.6 %collective-permute-start.11 = (bf16[8,2816]{1,0:T(8,128)(2,1)S(1)}, bf16[8,2816]{1,0:T(8,128)(2,1)S(1)}, u32[]{:S(2)}, u32[]{:S(2)}) collective-permute-start(bf16[8,2816]{1,0:T(8,128)(2,1)S(1)} %slice.4), channel_id=1, source_target_pairs={{0,1},{1,2},{2,3},{4,5},{5,6},{6,7},{8,9},{9,10},{10,11},{12,13},{... | collective-permute-start | bytes 135176 | tf_op jit(solution)/shard_map/ppermute | solution.py:22
  9.9 0.8 %copy.18 = bf16[1,1,16,8,2,32]{2,5,3,4,1,0:T(8,128)(2,1)} copy(bf16[1,1,16,8,2,32]{5,4,3,2,1,0:T(2,128)(2,1)S(1)} %bitcast.28) | data formatting | bytes 32768 | tf_op jit(solution)/shard_map/stack | solution.py:374
  11.2 0.8 %copy.20 = bf16[1,1,16,8,2,32]{2,5,3,4,1,0:T(8,128)(2,1)} copy(bf16[1,1,16,8,2,32]{5,4,3,2,1,0:T(2,128)(2,1)S(1)} %bitcast.29) | data formatting | bytes 32768 | tf_op jit(solution)/shard_map/stack | solution.py:374
  12.0 0.8 %copy.19 = bf16[1,1,16,8,2,32]{2,5,3,4,1,0:T(8,128)(2,1)} copy(bf16[1,1,16,8,2,32]{5,4,3,2,1,0:T(2,128)(2,1)S(1)} %bitcast.27) | data formatting | bytes 32768 | tf_op jit(solution)/shard_map/stack | solution.py:374
  12.8 6.4 %correlator_spectra.1 = (bf16[8,5632]{1,0:T(8,128)(2,1)S(1)}, bf16[8,5632]{1,0:T(8,128)(2,1)S(1)}, bf16[8,5632]{1,0:T(8,128)(2,1)S(1)}, bf16[8,5632]{1,0:T(8,128...) custom-call(s32[1]{0:T(128)} %bitcast.me_ref, ...), custom_call_target="tpu_custom_call" | custom-call | flops 10000000000 | bytes 4000000 | tf_op jit(solution)/shard_map/correlator_spectra/pallas_call | solution.py:239
  19.8 1.5 %collective-permute-start.1 = (bf16[8,5632]{1,0:T(8,128)(2,1)S(1)}, bf16[8,5632]{1,0:T(8,128)(2,1)S(1)}, u32[]{:S(2)}, u32[]{:S(2)}) collective-permute-start(bf16[8,5632]{1,0:T(8,128)(2,1)S(1)} %get-tuple-element.19), channel_id=1, source_target_pairs={{0,4},{4,0},{8,12},{12,8},{16,20},{20,16},{24,28},{28,24},{1,5},{5... | collective-permute-start | bytes 270344 | tf_op jit(solution)/shard_map/ppermute | solution.py:384
  21.2 1.6 %collective-permute-start.2 = (bf16[8,5632]{1,0:T(8,128)(2,1)S(1)}, bf16[8,5632]{1,0:T(8,128)(2,1)S(1)}, u32[]{:S(2)}, u32[]{:S(2)}) collective-permute-start(bf16[8,5632]{1,0:T(8,128)(2,1)S(1)} %get-tuple-element.20), channel_id=1, source_target_pairs={{0,8},{4,12},{8,0},{12,4},{16,24},{20,28},{24,16},{28,20},{1,9},{5... | collective-permute-start | bytes 270344 | tf_op jit(solution)/shard_map/ppermute | solution.py:384
  24.5 2.6 %collective-permute-start.4 = (bf16[8,5632]{1,0:T(8,128)(2,1)S(1)}, bf16[8,5632]{1,0:T(8,128)(2,1)S(1)}, u32[]{:S(2)}, u32[]{:S(2)}) collective-permute-start(bf16[8,5632]{1,0:T(8,128)(2,1)S(1)} %get-tuple-element.22), channel_id=1, source_target_pairs={{0,16},{4,20},{8,24},{12,28},{16,0},{20,4},{24,8},{28,12},{1,17},{... | collective-permute-start | bytes 270344 | tf_op jit(solution)/shard_map/ppermute | solution.py:384
  27.1 1.3 %collective-permute-start.5 = (bf16[8,5632]{1,0:T(8,128)(2,1)S(1)}, bf16[8,5632]{1,0:T(8,128)(2,1)S(1)}, u32[]{:S(2)}, u32[]{:S(2)}) collective-permute-start(bf16[8,5632]{1,0:T(8,128)(2,1)S(1)} %get-tuple-element.23), channel_id=1, source_target_pairs={{0,20},{4,16},{8,28},{12,24},{16,4},{20,0},{24,12},{28,8},{1,21},{... | collective-permute-start | bytes 270344 | tf_op jit(solution)/shard_map/ppermute | solution.py:384
  28.4 3.6 %collective-permute-start.6 = (bf16[8,5632]{1,0:T(8,128)(2,1)S(1)}, bf16[8,5632]{1,0:T(8,128)(2,1)S(1)}, u32[]{:S(2)}, u32[]{:S(2)}) collective-permute-start(bf16[8,5632]{1,0:T(8,128)(2,1)S(1)} %get-tuple-element.24), channel_id=1, source_target_pairs={{0,24},{4,28},{8,16},{12,20},{16,8},{20,12},{24,0},{28,4},{1,25},{... | collective-permute-start | bytes 270344 | tf_op jit(solution)/shard_map/ppermute | solution.py:384
  32.2 2.4 %pulsar_spectra.1 = (bf16[32,1408]{1,0:T(8,128)(2,1)S(1)}, bf16[32,1408]{1,0:T(8,128)(2,1)S(1)}, bf16[32,1408]{1,0:T(8,128)(2,1)S(1)}, bf16[32,1408]{1,0:T(8,128...) custom-call(s32[1]{0:T(128)} %bitcast.me_ref, ...), custom_call_target="tpu_custom_call" | custom-call | flops 5000000000 | bytes 2000000 | tf_op jit(solution)/shard_map/pulsar_spectra/pallas_call | solution.py:141
  34.6 1.5 %collective-permute-start.12 = (bf16[32,1408]{1,0:T(8,128)(2,1)S(1)}, bf16[32,1408]{1,0:T(8,128)(2,1)S(1)}, u32[]{:S(2)}, u32[]{:S(2)}) collective-permute-start(bf16[32,1408]{1,0:T(8,128)(2,1)S(1)} %get-tuple-element.27), channel_id=1, source_target_pairs={{0,4},{4,0},{8,12},{12,8},{16,20},{20,16},{24,28},{28,24},{1,5},{5... | collective-permute-start | bytes 270344 | tf_op jit(solution)/shard_map/ppermute | solution.py:384
  36.2 2.9 %collective-permute-start.13 = (bf16[32,1408]{1,0:T(8,128)(2,1)S(1)}, bf16[32,1408]{1,0:T(8,128)(2,1)S(1)}, u32[]{:S(2)}, u32[]{:S(2)}) collective-permute-start(bf16[32,1408]{1,0:T(8,128)(2,1)S(1)} %get-tuple-element.28), channel_id=1, source_target_pairs={{0,8},{4,12},{8,0},{12,4},{16,24},{20,28},{24,16},{28,20},{1,9},{5... | collective-permute-start | bytes 270344 | tf_op jit(solution)/shard_map/ppermute | solution.py:384
  39.1 2.4 %collective-permute-done.5.refs_5_ = bf16[8,5632]{1,0:T(8,128)(2,1)S(1)} collective-permute-done((bf16[8,5632]{1,0:T(8,128)(2,1)S(1)}, bf16[8,5632]{1,0:T(8,128)(2,1)S(1)}, u32[]{:S(2)}, u32[]{:S(2)}) %collective-permute-start.5) | collective-permute-done | bytes 90144 | tf_op jit(solution)/shard_map/ppermute | solution.py:384
  42.1 3.4 %collective-permute-start.15 = (bf16[32,1408]{1,0:T(8,128)(2,1)S(1)}, bf16[32,1408]{1,0:T(8,128)(2,1)S(1)}, u32[]{:S(2)}, u32[]{:S(2)}) collective-permute-start(bf16[32,1408]{1,0:T(8,128)(2,1)S(1)} %get-tuple-element.30), channel_id=1, source_target_pairs={{0,16},{4,20},{8,24},{12,28},{16,0},{20,4},{24,8},{28,12},{1,17},{... | collective-permute-start | bytes 270344 | tf_op jit(solution)/shard_map/ppermute | solution.py:384
  45.6 2.8 %collective-permute-start.16 = (bf16[32,1408]{1,0:T(8,128)(2,1)S(1)}, bf16[32,1408]{1,0:T(8,128)(2,1)S(1)}, u32[]{:S(2)}, u32[]{:S(2)}) collective-permute-start(bf16[32,1408]{1,0:T(8,128)(2,1)S(1)} %get-tuple-element.31), channel_id=1, source_target_pairs={{0,20},{4,16},{8,28},{12,24},{16,4},{20,0},{24,12},{28,8},{1,21},{... | collective-permute-start | bytes 270344 | tf_op jit(solution)/shard_map/ppermute | solution.py:384
  48.7 1.2 %collective-permute-start.17 = (bf16[32,1408]{1,0:T(8,128)(2,1)S(1)}, bf16[32,1408]{1,0:T(8,128)(2,1)S(1)}, u32[]{:S(2)}, u32[]{:S(2)}) collective-permute-start(bf16[32,1408]{1,0:T(8,128)(2,1)S(1)} %get-tuple-element.32), channel_id=1, source_target_pairs={{0,24},{4,28},{8,16},{12,20},{16,8},{20,12},{24,0},{28,4},{1,25},{... | collective-permute-start | bytes 270344 | tf_op jit(solution)/shard_map/ppermute | solution.py:384
  49.9 4.4 %collective-permute-start.18 = (bf16[32,1408]{1,0:T(8,128)(2,1)S(1)}, bf16[32,1408]{1,0:T(8,128)(2,1)S(1)}, u32[]{:S(2)}, u32[]{:S(2)}) collective-permute-start(bf16[32,1408]{1,0:T(8,128)(2,1)S(1)} %get-tuple-element.33), channel_id=1, source_target_pairs={{0,28},{4,24},{8,20},{12,16},{16,12},{20,8},{24,4},{28,0},{1,29},{... | collective-permute-start | bytes 270344 | tf_op jit(solution)/shard_map/ppermute | solution.py:384
  54.4 2.5 %collective-permute-start.9 = (f32[16,64]{1,0:T(8,128)S(1)}, f32[16,64]{1,0:T(8,128)S(1)}, u32[]{:S(2)}, u32[]{:S(2)}) collective-permute-start(f32[16,64]{1,0:T(8,128)S(1)} %get-tuple-element.37), channel_id=1, source_target_pairs={{0,2},{1,3},{2,0},{3,1},{4,6},{5,7},{6,4},{7,5},{8,10},{9,11},{10,... | collective-permute-start | bytes 12296 | tf_op jit(solution)/shard_map/ppermute | solution.py:407
  56.9 2.3 %collective-permute-done.16.refs_5_ = bf16[32,1408]{1,0:T(8,128)(2,1)S(1)} collective-permute-done((bf16[32,1408]{1,0:T(8,128)(2,1)S(1)}, bf16[32,1408]{1,0:T(8,128)(2,1)S(1)}, u32[]{:S(2)}, u32[]{:S(2)}) %collective-permute-start.16) | collective-permute-done | bytes 90144 | tf_op jit(solution)/shard_map/ppermute | solution.py:384
  59.2 2.3 %beam_former.1 = f32[512,176]{1,0:T(8,128)} custom-call(s32[1]{0:T(128)} %bitcast.me_ref, bf16[2,512,32]{2,1,0:T(8,128)(2,1)S(1)} %copy.22.weight_ref, bf16[32,1408]{1,0:T(8,128)(2,1)S(1)} %get-tuple-element.26.refs_0_, bf16[32,1408]{1,0:T(8,128)(2,1)S(1)} %collective-permute-done.12.refs_1_, bf16[32,1408]{1,0:T(8,128)(2,1)S(1)} %collective-permute-done.13.refs_2_, ...), custom_call_target="tpu_custom_call" | custom-call | flops 4000000000 | bytes 2000000 | tf_op jit(solution)/shard_map/beam_former/pallas_call | solution.py:294
  61.5 0.8 %finish.1 = f32[1,8,2,32]{3,2,1,0:T(2,128)} custom-call(s32[1]{0:T(128)} %bitcast.me_ref, f32[16,64]{1,0:T(8,128)S(1)} %get-tuple-element.39.refs_0_, f32[16,64]{1,0:T(8,128)S(1)} %collective-permute-done.8.refs_1_, f32[16,64]{1,0:T(8,128)S(1)} %collective-permute-done.9.refs_2_, f32[16,64]{1,0:T(8,128)S(1)} %collective-permute-done.10.refs_3_), custom_call_target="tpu_custom_call" | custom-call | tf_op jit(solution)/shard_map/finish/pallas_call | solution.py:351
  (58 shorter events, 4.7 us)
Async XLA Ops:
  0.6 12.1 %copy-start.7 = (f32[256,128]{1,0:T(8,128)S(1)}, f32[256,128]{1,0:T(8,128)}, u32[]{:S(2)}) copy-start(f32[256,128]{1,0:T(8,128)} %constant.87.clone.sin_ref) | copy-start | bytes 393220
  2.1 10.6 %collective-permute-start = (bf16[8,45056]{1,0:T(8,128)(2,1)S(1)}, bf16[8,45056]{1,0:T(8,128)(2,1)S(1)}, u32[]{:S(2)}, u32[]{:S(2)}) collective-permute-start(bf16[8,45056]{1,0:T(8,128)(2,1)S(1)} %reshape.34.own_ref), channel_id=1, source_target_pairs={{0,1},{1,2},{2,3},{4,5},{5,6},{6,7},{8,9},{9,10},{10,11},{12,13},{... | collective-permute-start | bytes 2162696 | tf_op jit(solution)/shard_map/ppermute | solution.py:22
  4.6 22.5 %collective-permute-start.11 = (bf16[8,2816]{1,0:T(8,128)(2,1)S(1)}, bf16[8,2816]{1,0:T(8,128)(2,1)S(1)}, u32[]{:S(2)}, u32[]{:S(2)}) collective-permute-start(bf16[8,2816]{1,0:T(8,128)(2,1)S(1)} %slice.4), channel_id=1, source_target_pairs={{0,1},{1,2},{2,3},{4,5},{5,6},{6,7},{8,9},{9,10},{10,11},{12,13},{... | collective-permute-start | bytes 135176 | tf_op jit(solution)/shard_map/ppermute | solution.py:22
  12.8 10.1 %copy-start.10 = (bf16[1,1,16,8,2,32]{2,5,3,4,1,0:T(8,128)(2,1)S(1)}, bf16[1,1,16,8,2,32]{2,5,3,4,1,0:T(8,128)(2,1)}, u32[]{:S(2)}) copy-start(bf16[1,1,16,8,2,32]{2,5,3,4,1,0:T(8,128)(2,1)} %copy.18) | copy-start | bytes 49156
  12.8 10.1 %copy-start.11 = (bf16[1,1,16,8,2,32]{2,5,3,4,1,0:T(8,128)(2,1)S(1)}, bf16[1,1,16,8,2,32]{2,5,3,4,1,0:T(8,128)(2,1)}, u32[]{:S(2)}) copy-start(bf16[1,1,16,8,2,32]{2,5,3,4,1,0:T(8,128)(2,1)} %copy.20) | copy-start | bytes 49156
  12.8 10.1 %copy-start.12 = (bf16[1,1,16,8,2,32]{2,5,3,4,1,0:T(8,128)(2,1)S(1)}, bf16[1,1,16,8,2,32]{2,5,3,4,1,0:T(8,128)(2,1)}, u32[]{:S(2)}) copy-start(bf16[1,1,16,8,2,32]{2,5,3,4,1,0:T(8,128)(2,1)} %copy.19) | copy-start | bytes 49156
  19.8 8.6 %collective-permute-start.1 = (bf16[8,5632]{1,0:T(8,128)(2,1)S(1)}, bf16[8,5632]{1,0:T(8,128)(2,1)S(1)}, u32[]{:S(2)}, u32[]{:S(2)}) collective-permute-start(bf16[8,5632]{1,0:T(8,128)(2,1)S(1)} %get-tuple-element.19), channel_id=1, source_target_pairs={{0,4},{4,0},{8,12},{12,8},{16,20},{20,16},{24,28},{28,24},{1,5},{5... | collective-permute-start | bytes 270344 | tf_op jit(solution)/shard_map/ppermute | solution.py:384
  21.2 10.7 %collective-permute-start.2 = (bf16[8,5632]{1,0:T(8,128)(2,1)S(1)}, bf16[8,5632]{1,0:T(8,128)(2,1)S(1)}, u32[]{:S(2)}, u32[]{:S(2)}) collective-permute-start(bf16[8,5632]{1,0:T(8,128)(2,1)S(1)} %get-tuple-element.20), channel_id=1, source_target_pairs={{0,8},{4,12},{8,0},{12,4},{16,24},{20,28},{24,16},{28,20},{1,9},{5... | collective-permute-start | bytes 270344 | tf_op jit(solution)/shard_map/ppermute | solution.py:384
  24.1 10.6 %collective-permute-start.3 = (bf16[8,5632]{1,0:T(8,128)(2,1)S(1)}, bf16[8,5632]{1,0:T(8,128)(2,1)S(1)}, u32[]{:S(2)}, u32[]{:S(2)}) collective-permute-start(bf16[8,5632]{1,0:T(8,128)(2,1)S(1)} %get-tuple-element.21), channel_id=1, source_target_pairs={{0,12},{4,8},{8,4},{12,0},{16,28},{20,24},{24,20},{28,16},{1,13},{... | collective-permute-start | bytes 270344 | tf_op jit(solution)/shard_map/ppermute | solution.py:384
  24.5 11.6 %collective-permute-start.4 = (bf16[8,5632]{1,0:T(8,128)(2,1)S(1)}, bf16[8,5632]{1,0:T(8,128)(2,1)S(1)}, u32[]{:S(2)}, u32[]{:S(2)}) collective-permute-start(bf16[8,5632]{1,0:T(8,128)(2,1)S(1)} %get-tuple-element.22), channel_id=1, source_target_pairs={{0,16},{4,20},{8,24},{12,28},{16,0},{20,4},{24,8},{28,12},{1,17},{... | collective-permute-start | bytes 270344 | tf_op jit(solution)/shard_map/ppermute | solution.py:384
  27.1 14.3 %collective-permute-start.5 = (bf16[8,5632]{1,0:T(8,128)(2,1)S(1)}, bf16[8,5632]{1,0:T(8,128)(2,1)S(1)}, u32[]{:S(2)}, u32[]{:S(2)}) collective-permute-start(bf16[8,5632]{1,0:T(8,128)(2,1)S(1)} %get-tuple-element.23), channel_id=1, source_target_pairs={{0,20},{4,16},{8,28},{12,24},{16,4},{20,0},{24,12},{28,8},{1,21},{... | collective-permute-start | bytes 270344 | tf_op jit(solution)/shard_map/ppermute | solution.py:384
  28.4 13.7 %collective-permute-start.6 = (bf16[8,5632]{1,0:T(8,128)(2,1)S(1)}, bf16[8,5632]{1,0:T(8,128)(2,1)S(1)}, u32[]{:S(2)}, u32[]{:S(2)}) collective-permute-start(bf16[8,5632]{1,0:T(8,128)(2,1)S(1)} %get-tuple-element.24), channel_id=1, source_target_pairs={{0,24},{4,28},{8,16},{12,20},{16,8},{20,12},{24,0},{28,4},{1,25},{... | collective-permute-start | bytes 270344 | tf_op jit(solution)/shard_map/ppermute | solution.py:384
  32.0 16.4 %copy-start.9 = (bf16[8,5632]{1,0:T(8,128)(2,1)S(1)}, bf16[8,5632]{1,0:T(8,128)(2,1)}, u32[]{:S(2)}) copy-start(bf16[8,5632]{1,0:T(8,128)(2,1)} %copy-done.8) | copy-start | bytes 270340
  32.0 13.6 %collective-permute-start.7 = (bf16[8,5632]{1,0:T(8,128)(2,1)S(1)}, bf16[8,5632]{1,0:T(8,128)(2,1)S(1)}, u32[]{:S(2)}, u32[]{:S(2)}) collective-permute-start(bf16[8,5632]{1,0:T(8,128)(2,1)S(1)} %get-tuple-element.25), channel_id=1, source_target_pairs={{0,28},{4,24},{8,20},{12,16},{16,12},{20,8},{24,4},{28,0},{1,29},{... | collective-permute-start | bytes 270344 | tf_op jit(solution)/shard_map/ppermute | solution.py:384
  34.6 14.0 %collective-permute-start.12 = (bf16[32,1408]{1,0:T(8,128)(2,1)S(1)}, bf16[32,1408]{1,0:T(8,128)(2,1)S(1)}, u32[]{:S(2)}, u32[]{:S(2)}) collective-permute-start(bf16[32,1408]{1,0:T(8,128)(2,1)S(1)} %get-tuple-element.27), channel_id=1, source_target_pairs={{0,4},{4,0},{8,12},{12,8},{16,20},{20,16},{24,28},{28,24},{1,5},{5... | collective-permute-start | bytes 270344 | tf_op jit(solution)/shard_map/ppermute | solution.py:384
  36.2 13.7 %collective-permute-start.13 = (bf16[32,1408]{1,0:T(8,128)(2,1)S(1)}, bf16[32,1408]{1,0:T(8,128)(2,1)S(1)}, u32[]{:S(2)}, u32[]{:S(2)}) collective-permute-start(bf16[32,1408]{1,0:T(8,128)(2,1)S(1)} %get-tuple-element.28), channel_id=1, source_target_pairs={{0,8},{4,12},{8,0},{12,4},{16,24},{20,28},{24,16},{28,20},{1,9},{5... | collective-permute-start | bytes 270344 | tf_op jit(solution)/shard_map/ppermute | solution.py:384
  41.5 12.9 %collective-permute-start.14 = (bf16[32,1408]{1,0:T(8,128)(2,1)S(1)}, bf16[32,1408]{1,0:T(8,128)(2,1)S(1)}, u32[]{:S(2)}, u32[]{:S(2)}) collective-permute-start(bf16[32,1408]{1,0:T(8,128)(2,1)S(1)} %get-tuple-element.29), channel_id=1, source_target_pairs={{0,12},{4,8},{8,4},{12,0},{16,28},{20,24},{24,20},{28,16},{1,13},{... | collective-permute-start | bytes 270344 | tf_op jit(solution)/shard_map/ppermute | solution.py:384
  42.1 12.3 %collective-permute-start.15 = (bf16[32,1408]{1,0:T(8,128)(2,1)S(1)}, bf16[32,1408]{1,0:T(8,128)(2,1)S(1)}, u32[]{:S(2)}, u32[]{:S(2)}) collective-permute-start(bf16[32,1408]{1,0:T(8,128)(2,1)S(1)} %get-tuple-element.30), channel_id=1, source_target_pairs={{0,16},{4,20},{8,24},{12,28},{16,0},{20,4},{24,8},{28,12},{1,17},{... | collective-permute-start | bytes 270344 | tf_op jit(solution)/shard_map/ppermute | solution.py:384
  45.6 13.6 %collective-permute-start.16 = (bf16[32,1408]{1,0:T(8,128)(2,1)S(1)}, bf16[32,1408]{1,0:T(8,128)(2,1)S(1)}, u32[]{:S(2)}, u32[]{:S(2)}) collective-permute-start(bf16[32,1408]{1,0:T(8,128)(2,1)S(1)} %get-tuple-element.31), channel_id=1, source_target_pairs={{0,20},{4,16},{8,28},{12,24},{16,4},{20,0},{24,12},{28,8},{1,21},{... | collective-permute-start | bytes 270344 | tf_op jit(solution)/shard_map/ppermute | solution.py:384
  48.7 10.5 %collective-permute-start.17 = (bf16[32,1408]{1,0:T(8,128)(2,1)S(1)}, bf16[32,1408]{1,0:T(8,128)(2,1)S(1)}, u32[]{:S(2)}, u32[]{:S(2)}) collective-permute-start(bf16[32,1408]{1,0:T(8,128)(2,1)S(1)} %get-tuple-element.32), channel_id=1, source_target_pairs={{0,24},{4,28},{8,16},{12,20},{16,8},{20,12},{24,0},{28,4},{1,25},{... | collective-permute-start | bytes 270344 | tf_op jit(solution)/shard_map/ppermute | solution.py:384
  49.9 9.3 %collective-permute-start.18 = (bf16[32,1408]{1,0:T(8,128)(2,1)S(1)}, bf16[32,1408]{1,0:T(8,128)(2,1)S(1)}, u32[]{:S(2)}, u32[]{:S(2)}) collective-permute-start(bf16[32,1408]{1,0:T(8,128)(2,1)S(1)} %get-tuple-element.33), channel_id=1, source_target_pairs={{0,28},{4,24},{8,20},{12,16},{16,12},{20,8},{24,4},{28,0},{1,29},{... | collective-permute-start | bytes 270344 | tf_op jit(solution)/shard_map/ppermute | solution.py:384
  54.3 7.2 %collective-permute-start.8 = (f32[16,64]{1,0:T(8,128)S(1)}, f32[16,64]{1,0:T(8,128)S(1)}, u32[]{:S(2)}, u32[]{:S(2)}) collective-permute-start(f32[16,64]{1,0:T(8,128)S(1)} %get-tuple-element.38), channel_id=1, source_target_pairs={{0,1},{1,2},{2,3},{3,0},{4,5},{5,6},{6,7},{7,4},{8,9},{9,10},{10,1... | collective-permute-start | bytes 12296 | tf_op jit(solution)/shard_map/ppermute | solution.py:407
  54.4 7.1 %collective-permute-start.9 = (f32[16,64]{1,0:T(8,128)S(1)}, f32[16,64]{1,0:T(8,128)S(1)}, u32[]{:S(2)}, u32[]{:S(2)}) collective-permute-start(f32[16,64]{1,0:T(8,128)S(1)} %get-tuple-element.37), channel_id=1, source_target_pairs={{0,2},{1,3},{2,0},{3,1},{4,6},{5,7},{6,4},{7,5},{8,10},{9,11},{10,... | collective-permute-start | bytes 12296 | tf_op jit(solution)/shard_map/ppermute | solution.py:407
  59.2 2.3 %collective-permute-start.10 = (f32[16,64]{1,0:T(8,128)S(1)}, f32[16,64]{1,0:T(8,128)S(1)}, u32[]{:S(2)}, u32[]{:S(2)}) collective-permute-start(f32[16,64]{1,0:T(8,128)S(1)} %get-tuple-element.36), channel_id=1, source_target_pairs={{0,3},{1,0},{2,1},{3,2},{4,7},{5,4},{6,5},{7,6},{8,11},{9,8},{10,9... | collective-permute-start | bytes 12296 | tf_op jit(solution)/shard_map/ppermute | solution.py:407
  (9 other events, 48.2 us)
